TPU v7x, 256 devices: a whole 4x4x8 slice. The times are simulated.
256 devices in a mesh: gx: 32 (over x, y, core), gy: 8 (over z).
Axes of the slice: x: 4, y: 4, z: 8, core: 2. Of those that a mesh axis runs over, the one named last changes fastest.
Arguments:
- right_side: float32 [64, 32768], P(None, ('gx', 'gy')), may hold values from -14 to 14
- pressure_head: float32 [64, 32768], P(None, ('gx', 'gy')), may hold values from -3 to -0.1
- vg_alpha: float32 [32768], P(('gx', 'gy')), may hold values from 0.5 to 5
- live_counts: int32 [256], P(('gx', 'gy')), may hold values from 16 to 128, as said below
- partners: int32 [4, 32768], P(None, ('gx', 'gy')), may hold values from 0 to 127, as said below
- element_blocks: bfloat16 [64, 64, 32768], P(None, None, ('gx', 'gy')), may hold values from -1.5 to 9
- face_blocks: bfloat16 [4, 64, 64, 32768], P(None, None, None, ('gx', 'gy')), may hold values from -1 to 1
- local_inverse: bfloat16 [64, 64, 32768], P(None, None, ('gx', 'gy')), may hold values from -0.11 to 0.27
- coarse_basis: bfloat16 [64, 64, 32768], P(None, None, ('gx', 'gy')), may hold values from -0.125 to 0.125
- coarse_inverse: bfloat16 [16384, 16384], P(('gx', 'gy')), may hold values from -1 to 1, as said below
Outputs:
- update: float32 [64, 32768], P(None, ('gx', 'gy'))
- hessenberg: float32 [3, 2], replicated
Inputs may be any that keep to these rules, and one draw needn't show every extreme that they name: `live_counts`: some subdomain has all 128 slots live. `partners`: each partner is a live slot of the neighbouring subdomain when that subdomain exists. coarse_inverse is symmetric.
All inputs are finite; a program needn't handle non-finite values.
Results may differ from a plain program's by a relative error of at most 0.0003.
Values sent between devices are 32-bit elements; how exact they have to be, the bound alone decides.
No kernel may reach another device: no remote copies, remote signals or barrier semaphores. Data moves between devices by JAX's collectives and lax.ppermute only.
A program may use at most 128 MiB of HBM per device.

v0:
```python
import jax
import jax.numpy as jnp
from jax import lax
from jax.sharding import PartitionSpec as P

highest = lax.Precision.HIGHEST
shape_exponent = 1.6
time_factor = 4.0


def with_halo(cells, sides, width):
    for axis, dim in sides:
        count = lax.axis_size(axis)
        ends = count - 1
        head = lax.slice_in_dim(cells, 0, width, axis=dim)
        tail = lax.slice_in_dim(cells, cells.shape[dim] - width, cells.shape[dim], axis=dim)
        cells = jnp.concatenate(
            [
                lax.ppermute(tail, axis, [(i, (i + 1) % count) for i in range(ends)]),
                cells,
                lax.ppermute(head, axis, [((i + 1) % count, i) for i in range(ends)]),
            ],
            axis=dim,
        )
    return cells


def capacity(pressure, alpha_row):
    scaled = jnp.abs(alpha_row[None, :] * pressure)
    expo_m = 1.0 - 1.0 / shape_exponent
    return (
        time_factor
        * alpha_row[None, :]
        * shape_exponent
        * expo_m
        * jnp.power(scaled, shape_exponent - 1.0)
        * jnp.power(1.0 + jnp.power(scaled, shape_exponent), -(expo_m + 1.0))
    )


def apply_blocks(blocks, vector_in):
    return jnp.einsum("ije,je->ie", blocks.astype(jnp.float32), vector_in, precision=highest)


def shards(
    right_side,
    pressure_head,
    vg_alpha,
    live_counts,
    partners,
    element_blocks,
    face_blocks,
    local_inverse,
    coarse_basis,
    coarse_inverse,
):
    slot_total = right_side.shape[1]
    slot_ids = jnp.arange(slot_total, dtype=jnp.int32)
    live_mask = (slot_ids < live_counts[0]).astype(jnp.float32)[None, :]
    storage = capacity(pressure_head, vg_alpha)
    basis_float = coarse_basis.astype(jnp.float32)
    rhs_live = right_side * live_mask
    start_size = jnp.sqrt(lax.psum(jnp.sum(rhs_live * rhs_live), ("gx", "gy")))
    krylov = [rhs_live / start_size]
    directions = []
    columns = []
    for sweep in range(2):
        precondition_vector_in = krylov[-1]
        restricted = jnp.einsum("mje,je->m", basis_float, precondition_vector_in, precision=highest)
        precondition_coarse_part = jnp.dot(
            coarse_inverse.astype(jnp.float32),
            lax.all_gather(restricted, ("gx", "gy"), axis=0, tiled=True),
            precision=highest,
        )
        local_part = apply_blocks(local_inverse, precondition_vector_in)
        prolonged = jnp.einsum(
            "mje,m->je", basis_float, precondition_coarse_part, precision=highest
        )
        prepared = (local_part + prolonged) * live_mask
        directions.append(prepared)
        framed = with_halo(prepared[:, None, None, :], (("gx", 1), ("gy", 2)), 1)
        sources = (framed[:, 0, 1, :], framed[:, 2, 1, :], framed[:, 1, 0, :], framed[:, 1, 2, :])
        summed = apply_blocks(element_blocks, prepared) + storage * prepared
        for direction in range(4):
            picked = jnp.take(sources[direction], partners[direction], axis=1)
            summed = summed + apply_blocks(face_blocks[direction], picked)
        mapped = summed * live_mask
        partials = [jnp.sum(mapped * member) for member in krylov]
        coeffs = lax.psum(jnp.stack(partials), ("gx", "gy"))
        remains = mapped
        for position, member in enumerate(krylov):
            remains = remains - coeffs[position] * member
        height = jnp.sqrt(lax.psum(jnp.sum(remains * remains), ("gx", "gy")))
        coeffs, height, remains = (coeffs, height, remains)
        columns.append((coeffs, height))
        if sweep == 0:
            krylov.append(remains / height)
    h_one_one = columns[0][0][0]
    h_two_one = columns[0][1]
    h_one_two = columns[1][0][0]
    h_two_two = columns[1][0][1]
    h_three_two = columns[1][1]
    zero_entry = jnp.zeros((), jnp.float32)
    hessenberg = jnp.stack(
        [
            jnp.stack([h_one_one, h_one_two]),
            jnp.stack([h_two_one, h_two_two]),
            jnp.stack([zero_entry, h_three_two]),
        ]
    )
    gram_aa = h_one_one * h_one_one + h_two_one * h_two_one
    gram_ab = h_one_one * h_one_two + h_two_one * h_two_two
    gram_bb = h_one_two * h_one_two + h_two_two * h_two_two + h_three_two * h_three_two
    target_a = start_size * h_one_one
    target_b = start_size * h_one_two
    determinant = gram_aa * gram_bb - gram_ab * gram_ab
    weight_one = (gram_bb * target_a - gram_ab * target_b) / determinant
    weight_two = (gram_aa * target_b - gram_ab * target_a) / determinant
    update = weight_one * directions[0] + weight_two * directions[1]
    return (update, hessenberg)


def solution(mesh):
    placed = (
        P(None, ("gx", "gy")),
        P(None, ("gx", "gy")),
        P(("gx", "gy")),
        P(("gx", "gy")),
        P(None, ("gx", "gy")),
        P(None, None, ("gx", "gy")),
        P(None, None, None, ("gx", "gy")),
        P(None, None, ("gx", "gy")),
        P(None, None, ("gx", "gy")),
        P(("gx", "gy"), None),
    )
    return jax.shard_map(
        shards, mesh=mesh, in_specs=placed, out_specs=(P(None, ("gx", "gy")), P()), check_vma=False
    )
```

profile of v0, /device:TPU:1, one launch (start us, length us, event | category | flops | bytes accessed | tf_op | source)
XLA Modules:
  0.0 963.1 jit_solution(11995120081625729352)
XLA Ops:
  9.7 81.4 %psum.35 = f32[]{:T(128)} all-reduce(f32[]{:T(128)} %multiply_reduce_fusion.5), channel_id=1, replica_groups=mesh['gx'=32,'gy'=8] {'gx','gy'}, use_global_device_ids=true, to_apply=%region_1.0 | all-reduce | flops 1 | bytes 8 | tf_op jit(solution)/shard_map/psum | solution.py:63
  91.9 2.5 convolution_bitcast_fusion.1
  96.0 4.5 copy.17
  101.2 4.6 slice_bitcast_fusion.3
  108.7 5.5 copy.32
  114.1 5.5 copy.35
  119.6 5.4 copy.26
  125.0 4.5 copy.29
  129.5 5.6 copy.23
  135.2 193.6 %all-reduce.5.cloned.1.call-done = f32[16384]{0:T(1024)} async-done(((f32[16384]{0:T(1024)}), f32[16384]{0:T(1024)}) %all-reduce.5.cloned.1.call-update) | async-done | bytes 65552
  328.8 2.6 convolution_bitcast_fusion.3
  332.5 2.6 collective-permute-start
  335.1 1.9 collective-permute-start.1
  337.1 4.0 fusion.10
  341.7 4.2 collective-permute-start.2
  348.6 4.0 fusion.11
  354.2 4.0 fusion.12
  359.7 4.0 fusion.13
  366.1 3.3 fusion.14
  370.9 76.3 %psum.36 = f32[1]{0:T(128)} all-reduce(f32[1]{0:T(128)} %bitcast.53), channel_id=1, replica_groups=mesh['gx'=32,'gy'=8] {'gx','gy'}, use_global_device_ids=true, to_apply=%region_3.5 | all-reduce | flops 1 | bytes 8 | tf_op jit(solution)/shard_map/psum | solution.py:89
  448.5 73.5 %psum.37 = f32[]{:T(128)} all-reduce(f32[]{:T(128)} %multiply_reduce_fusion.3), channel_id=1, replica_groups=mesh['gx'=32,'gy'=8] {'gx','gy'}, use_global_device_ids=true, to_apply=%region_5.7 | all-reduce | flops 1 | bytes 8 | tf_op jit(solution)/shard_map/psum | solution.py:93
  525.8 3.9 fusion.15
  531.7 228.4 %all-reduce.7.cloned.1.call-done = f32[16384]{0:T(1024)} async-done(((f32[16384]{0:T(1024)}), f32[16384]{0:T(1024)}) %all-reduce.7.cloned.1.call-update) | async-done | bytes 65552
  760.1 2.6 convolution_bitcast_fusion.2
  764.7 2.6 collective-permute-start.4
  769.2 3.3 fusion.16
  772.9 3.2 collective-permute-start.6
  779.2 3.4 fusion.17
  785.9 3.4 fusion.19
  793.2 76.6 %psum.38 = f32[2]{0:T(128)S(1)} all-reduce(f32[2]{0:T(128)S(1)} %pad_maximum_fusion.3), channel_id=1, replica_groups=mesh['gx'=32,'gy'=8] {'gx','gy'}, use_global_device_ids=true, to_apply=%region_8.10 | all-reduce | flops 2 | bytes 16 | tf_op jit(solution)/shard_map/psum | solution.py:89
  875.6 2.0 multiply_reduce_fusion
  878.9 74.1 %psum.39 = f32[]{:T(128)} all-reduce(f32[]{:T(128)} %multiply_reduce_fusion), channel_id=1, replica_groups=mesh['gx'=32,'gy'=8] {'gx','gy'}, use_global_device_ids=true, to_apply=%region_10.12 | all-reduce | flops 1 | bytes 8 | tf_op jit(solution)/shard_map/psum | solution.py:93
  (120 shorter events, 41.4 us)
Async XLA Ops:
  7.2 321.6 %copy-start = (bf16[64,16384]{1,0:T(8,128)(2,1)S(1)}, bf16[64,16384]{1,0:T(8,128)(2,1)}, u32[]{:S(2)}) copy-start(bf16[64,16384]{1,0:T(8,128)(2,1)} %param.21) | copy-start | bytes 6291460
  7.2 88.8 %copy-start.5 = (bf16[64,64,128]{2,1,0:T(8,128)(2,1)S(1)}, bf16[64,64,128]{2,1,0:T(8,128)(2,1)}, u32[]{:S(2)}) copy-start(bf16[64,64,128]{2,1,0:T(8,128)(2,1)} %param.19) | copy-start | bytes 3145732
  7.2 321.6 %all-reduce.5.cloned.1.call-start = ((), (), s32[]{:S(2)}) async-start(), calls=%async_computation | async-start | bytes 131072
  91.9 8.7 copy-start.18
  94.7 0.6 copy-start.7
  95.4 664.7 %all-reduce.7.cloned.1.call-start = ((), (), s32[]{:S(2)}) async-start(), calls=%async_computation.1 | async-start | bytes 131072
  101.2 4.7 copy-start.19
  101.2 5.2 copy-start.4
  129.5 5.6 copy-start.12
  129.5 201.9 %copy-start.1 = (bf16[64,64,128]{2,1,0:T(8,128)(2,1)S(1)}, bf16[64,64,128]{2,1,0:T(8,128)(2,1)}, u32[]{:S(2)}) copy-start(bf16[64,64,128]{2,1,0:T(8,128)(2,1)} %param.20) | copy-start | bytes 3145732
  332.5 8.5 collective-permute-start
  335.1 5.9 collective-permute-start.1
  341.7 16.4 %collective-permute-start.2 = (f32[64,3,1,128]{0,3,2,1:T(8,128)}, f32[64,3,1,128]{0,3,2,1:T(8,128)}, u32[]{:S(2)}, u32[]{:S(2)}) collective-permute-start(f32[64,3,1,128]{0,3,2,1:T(8,128)} %pad_maximum_fusion), channel_id=1, source_target_pairs={{0,1},{1,2},{2,3},{3,4},{4,5},{5,6},{6,7},{8,9},{9,10},{10,11},{11... | collective-permute-start | bytes 294920 | tf_op jit(solution)/shard_map/ppermute | solution.py:19
  345.9 17.9 %collective-permute-start.3 = (f32[64,3,1,128]{0,3,2,1:T(8,128)}, f32[64,3,1,128]{0,3,2,1:T(8,128)}, u32[]{:S(2)}, u32[]{:S(2)}) collective-permute-start(f32[64,3,1,128]{0,3,2,1:T(8,128)} %pad_maximum_fusion), channel_id=1, source_target_pairs={{1,0},{2,1},{3,2},{4,3},{5,4},{6,5},{7,6},{9,8},{10,9},{11,10},{12... | collective-permute-start | bytes 294920 | tf_op jit(solution)/shard_map/ppermute | solution.py:21
  352.5 7.1 copy-start.14
  359.7 9.6 %copy-start.8 = (f32[128,1,64]{2,1,0:T(1,128)S(1)}, f32[128,1,64]{2,1,0:T(1,128)}, u32[]{:S(2)}) copy-start(f32[128,1,64]{2,1,0:T(1,128)} %fusion.10) | copy-start | bytes 98308
  365.2 4.1 copy-start.9
  365.2 4.1 copy-start.10
  365.3 4.1 copy-start.11
  525.2 0.6 copy-start.6
  762.7 16.4 %copy-start.16 = (pred[128]{0:T(512)(128)(4,1)S(1)}, pred[128]{0:T(512)(128)(4,1)}, u32[]{:S(2)}) copy-start(pred[128]{0:T(512)(128)(4,1)} %get-tuple-element.10) | copy-start | bytes 388
  762.7 16.4 %copy-start.17 = (pred[128]{0:T(512)(128)(4,1)S(1)}, pred[128]{0:T(512)(128)(4,1)}, u32[]{:S(2)}) copy-start(pred[128]{0:T(512)(128)(4,1)} %get-tuple-element.22) | copy-start | bytes 388
  764.7 7.9 collective-permute-start.4
  767.3 5.6 collective-permute-start.5
  772.9 11.5 %collective-permute-start.6 = (f32[64,3,1,128]{0,3,2,1:T(8,128)S(1)}, f32[64,3,1,128]{0,3,2,1:T(8,128)S(1)}, u32[]{:S(2)}, u32[]{:S(2)}) collective-permute-start(f32[64,3,1,128]{0,3,2,1:T(8,128)S(1)} %pad_maximum_fusion.1), channel_id=1, source_target_pairs={{0,1},{1,2},{2,3},{3,4},{4,5},{5,6},{6,7},{8,9},{9,10},{10,11},{11... | collective-permute-start | bytes 294920 | tf_op jit(solution)/shard_map/ppermute | solution.py:19
  776.1 9.0 collective-permute-start.7
  779.1 3.6 copy-start.3
  782.6 3.1 copy-start.13
  782.7 3.1 copy-start.15
  785.7 3.6 copy-start.2
  785.9 5.2 copy-start.20
  785.9 5.2 copy-start.21
Sparse Core Ops, SparseCore 0:
  95.5 233.2 all-reduce.4
  526.0 234.1 all-reduce.6
where the time goes:
time: 967 us; the launch traced here: 963 us
  waiting for transfers between devices  422 us (44%)
  blocking collectives  382 us (40%)
  matrix products  49.4 us (5%)
  local copies, waits for them, and re-layouts  48 us (5%)
  between operations  24.9 us (3%)
  starting transfers between devices  19.8 us (2%)
  other arithmetic  16.8 us (2%)
    unnamed x4, waiting for transfers between devices  422 us
    psum x2, blocking collectives, shards(): coeffs = lax.psum(jnp.stack(partials), ('gx', 'gy'))  153 us
    psum x2, blocking collectives, shards(): height = jnp.sqrt(lax.psum(jnp.sum(remains * remains), ('gx', 'gy')))  148 us
    psum x1, blocking collectives, shards(): start_size = jnp.sqrt(lax.psum(jnp.sum(rhs_live * rhs_live), ('gx', 'gy')))  81.4 us
    dot_general x12, matrix products, apply_blocks(): jnp.einsum('ije,je->ie', blocks.astype(jnp.float32), vector_in, precision...  38.6 us
    squeeze x5, local copies, waits for them, and re-layouts, shards(): summed = summed + apply_blocks(face_blocks[direction], picked)  25.4 us
  transfers between devices with their start and end apart: 10, of which 3 were waited for; matrix products, arithmetic and copies ran while one was open for 8% of the time, Pallas kernels for 0%

commit v1 on v0

v1 whole, which is shorter than its diff:
```python
import jax
import jax.numpy as jnp
from jax import lax
from jax.experimental import pallas as pl
from jax.experimental.pallas import tpu as pltpu
from jax.sharding import PartitionSpec as P

shape_exponent = 1.6
time_factor = 4.0
expo_m = 1.0 - 1.0 / shape_exponent

NODES = 64
MODES = 64
SLOTS = 128
DOTS = 8
ROWS = MODES + DOTS
F32 = jnp.float32
VM = pl.BlockSpec(memory_space=pltpu.VMEM)
SM = pl.BlockSpec(memory_space=pltpu.SMEM)


def live_mask(count):
    slots = lax.broadcasted_iota(jnp.int32, (1, SLOTS), 1)
    return (slots < count).astype(F32)


def tile_sum(block):
    parts = [block[8 * t : 8 * t + 8] for t in range(8)]
    while len(parts) > 1:
        parts = [a + b for a, b in zip(parts[::2], parts[1::2])]
    return parts[0]


def fold_rows(partial_ref, rows):
    parts = [partial_ref[pl.ds(k, rows, stride=8), :] for k in range(8)]
    while len(parts) > 1:
        parts = [a + b for a, b in zip(parts[::2], parts[1::2])]
    return parts[0]


def blocks_into(partial_ref, terms):
    def body(i, carry):
        total = None
        for block_at, vector in terms:
            part = tile_sum(block_at(i).astype(F32) * vector())
            total = part if total is None else total + part
        partial_ref[pl.ds(pl.multiple_of(8 * i, 8), 8), :] = total
        return carry

    lax.fori_loop(0, NODES, body, 0, unroll=4)


def send_row(partial_ref, out_ref):
    square = jnp.concatenate(
        [fold_rows(partial_ref, ROWS), jnp.zeros((SLOTS - ROWS, SLOTS), F32)], axis=0
    )
    row = jnp.sum(square.T, axis=0, keepdims=True)
    out_ref[...] = jnp.broadcast_to(row, out_ref.shape)


def put_dots(partial_ref, pairs):
    for k in range(DOTS):
        rows = pl.ds(8 * (MODES + k), 8)
        if k < len(pairs):
            left, right = pairs[k]
            partial_ref[rows, :] = tile_sum(left * right)
        else:
            partial_ref[rows, :] = jnp.zeros((8, SLOTS), F32)


def restrict_kernel(count_ref, rhs_ref, basis_ref, row_ref, partial_ref):
    b = rhs_ref[...] * live_mask(count_ref[0])
    blocks_into(partial_ref, [(lambda m: basis_ref[m], lambda: b)])
    put_dots(partial_ref, [])
    send_row(partial_ref, row_ref)


def halves(rows_ref):
    lane = lax.broadcasted_iota(jnp.int32, (SLOTS, SLOTS), 1)
    even = rows_ref[pl.ds(0, SLOTS, stride=2), :]
    odd = rows_ref[pl.ds(1, SLOTS, stride=2), :]
    return jnp.where(lane < MODES, even, pltpu.roll(odd, MODES, 1))


def precondition(v_ref, coarse_ref, inverse_ref, local_ref, basis_ref, partial_ref, modal_ref):
    def coarse_step(t, acc):
        column = inverse_ref[:, pl.ds(pl.multiple_of(t * SLOTS, SLOTS), SLOTS)].astype(F32)
        return acc + column * coarse_ref[pl.ds(t, 1), :]

    acc = lax.fori_loop(0, 2 * MODES, coarse_step, jnp.zeros((MODES, SLOTS), F32), unroll=8)
    modal_ref[...] = jnp.broadcast_to(jnp.sum(acc, axis=1, keepdims=True), (MODES, SLOTS))
    blocks_into(partial_ref, [(lambda i: local_ref[i], lambda: v_ref[...])])

    def prolong_step(m, total):
        return total + basis_ref[m].astype(F32) * modal_ref[pl.ds(m, 1), :]

    total = lax.fori_loop(0, MODES, prolong_step, jnp.zeros((NODES, SLOTS), F32), unroll=8)
    return total + fold_rows(partial_ref, NODES)


def first_kernel(
    count_ref, rhs_ref, gathered_ref, inverse_ref, local_ref, basis_ref,
    z_ref, coarse_ref, b_ref, partial_ref, modal_ref,
):
    mask = live_mask(count_ref[0])
    coarse_ref[...] = halves(gathered_ref)
    b_ref[...] = rhs_ref[...] * mask
    z = precondition(b_ref, coarse_ref, inverse_ref, local_ref, basis_ref, partial_ref, modal_ref)
    z_ref[...] = z * mask


def lane_of(row, k):
    lane = lax.broadcasted_iota(jnp.int32, row.shape, 1)
    return jnp.sum(jnp.where(lane == k, row, 0.0), axis=1, keepdims=True)


def second_kernel(
    b_ref, w_ref, count_ref, coarse_ref, gathered_ref, inverse_ref, local_ref, basis_ref,
    z_ref, v_ref, sums_ref, mixed_ref, partial_ref, modal_ref,
):
    mask = live_mask(count_ref[0])
    sums = jnp.sum(gathered_ref[...], axis=0, keepdims=True)
    sums_ref[...] = jnp.broadcast_to(sums, sums_ref.shape)
    along = lane_of(sums, MODES) / lane_of(sums, MODES + 2)
    scale = 1.0 / jnp.sqrt(lane_of(sums, MODES + 1))
    mixed_ref[...] = (halves(gathered_ref) - along * coarse_ref[...]) * scale
    v_ref[...] = (w_ref[...] - along * b_ref[...]) * scale
    z = precondition(v_ref, mixed_ref, inverse_ref, local_ref, basis_ref, partial_ref, modal_ref)
    z_ref[...] = z * mask


def own_kernel(z_ref, blocks_ref, pressure_ref, alpha_ref, out_ref, partial_ref):
    blocks_into(partial_ref, [(lambda i: blocks_ref[i], lambda: z_ref[...])])
    alpha = alpha_ref[...]
    scaled = jnp.abs(alpha * pressure_ref[...])
    power = jnp.exp((shape_exponent - 1.0) * jnp.log(scaled))
    tail = jnp.exp(-(expo_m + 1.0) * jnp.log(1.0 + power * scaled))
    storage = (time_factor * shape_exponent * expo_m) * alpha * power * tail
    out_ref[...] = fold_rows(partial_ref, NODES) + storage * z_ref[...]


def faces_sum(own_ref, count_ref, faces_ref, partners_ref, source_refs, blocks_ref, picked_ref, partial_ref):
    for q, source_ref in enumerate(source_refs):
        slots = jnp.broadcast_to(partners_ref[pl.ds(faces_ref[q], 1), :], (NODES, SLOTS))
        picked_ref[q] = jnp.take_along_axis(source_ref[...], slots, axis=1)
    faces = [faces_ref[q] for q in range(4)]
    blocks_into(
        partial_ref,
        [(lambda i, q=q: blocks_ref[faces[q], i], lambda q=q: picked_ref[q]) for q in range(4)],
    )
    return (own_ref[...] + fold_rows(partial_ref, NODES)) * live_mask(count_ref[0])


def image_kernel(
    own_ref, count_ref, faces_ref, partners_ref, s0, s1, s2, s3, blocks_ref, b_ref, basis_ref,
    w_ref, row_ref, picked_ref, partial_ref,
):
    w_ref[...] = faces_sum(
        own_ref, count_ref, faces_ref, partners_ref, (s0, s1, s2, s3), blocks_ref, picked_ref, partial_ref
    )
    blocks_into(partial_ref, [(lambda m: basis_ref[m], lambda: w_ref[...])])
    w = w_ref[...]
    b = b_ref[...]
    put_dots(partial_ref, [(w, b), (w, w), (b, b)])
    send_row(partial_ref, row_ref)


def last_image_kernel(
    own_ref, count_ref, faces_ref, partners_ref, s0, s1, s2, s3, blocks_ref, b_ref, v_ref,
    row_ref, picked_ref, partial_ref,
):
    w = faces_sum(
        own_ref, count_ref, faces_ref, partners_ref, (s0, s1, s2, s3), blocks_ref, picked_ref, partial_ref
    )
    b = b_ref[...]
    v = v_ref[...]
    partial_ref[pl.ds(0, 8 * MODES), :] = jnp.zeros((8 * MODES, SLOTS), F32)
    put_dots(partial_ref, [(w, b), (w, v), (w, w), (v, v), (b, v)])
    send_row(partial_ref, row_ref)


def final_kernel(first_ref, gathered_ref, z1_ref, z2_ref, update_ref, hess_ref):
    sums = first_ref[0:1, :]
    late = jnp.sum(gathered_ref[...], axis=0, keepdims=True)
    wb, ww, bb = (lane_of(sums, MODES + k) for k in range(3))
    xb, xv, xx, vv, bv = (lane_of(late, MODES + k) for k in range(5))
    beta = jnp.sqrt(bb)
    size = jnp.sqrt(vv)
    h11 = wb / bb
    h21 = size * jnp.sqrt(ww) / beta
    h12 = xb / (size * beta)
    h22 = xv / vv
    cross = bv / (beta * size)
    rest = xx / vv - h12 * h12 - h22 * h22 + 2.0 * h12 * h22 * cross
    h32 = jnp.sqrt(jnp.maximum(rest, 0.0))
    gram_aa = h11 * h11 + h21 * h21
    gram_ab = h11 * h12 + h21 * h22
    gram_bb = h12 * h12 + h22 * h22 + h32 * h32
    target_a = beta * h11
    target_b = beta * h12
    determinant = gram_aa * gram_bb - gram_ab * gram_ab
    weight_one = (gram_bb * target_a - gram_ab * target_b) / determinant
    weight_two = (gram_aa * target_b - gram_ab * target_a) / determinant
    update_ref[...] = (weight_one / beta) * z1_ref[...] + (weight_two / size) * z2_ref[...]
    row = lax.broadcasted_iota(jnp.int32, (2, 3), 0)
    col = lax.broadcasted_iota(jnp.int32, (2, 3), 1)
    hess = jnp.where(row == 0, jnp.where(col == 0, h11, h21), jnp.where(col == 0, h12, jnp.where(col == 1, h22, h32)))
    hess_ref[...] = jnp.where((row == 0) & (col == 2), 0.0, hess)


def vec(*shape):
    return jax.ShapeDtypeStruct(shape, F32)


def call(body, name, specs, outs, scratch, megabytes=4):
    return pl.pallas_call(
        body,
        name=name,
        in_specs=specs,
        out_specs=jax.tree.map(lambda _: VM, outs),
        out_shape=outs,
        scratch_shapes=scratch,
        compiler_params=pltpu.CompilerParams(vmem_limit_bytes=megabytes << 20),
    )


def swaps(mesh_shape):
    n_gx, n_gy = mesh_shape
    at = lambda i, j: i * n_gy + j
    pairs = ([], [], [], [])
    for i in range(n_gx):
        for j in range(n_gy):
            if i + 1 < n_gx:
                pairs[i % 2] .extend([(at(i, j), at(i + 1, j)), (at(i + 1, j), at(i, j))])
            if j + 1 < n_gy:
                pairs[2 + j % 2].extend([(at(i, j), at(i, j + 1)), (at(i, j + 1), at(i, j))])
    return pairs


def solution(mesh):
    axes = ("gx", "gy")
    n_gx, n_gy = mesh.shape["gx"], mesh.shape["gy"]
    total = n_gx * n_gy
    pairs = swaps((n_gx, n_gy))

    def exchange(rows):
        return lax.all_to_all(rows, axes, 0, 0, tiled=True)

    def shards(
        right_side, pressure_head, vg_alpha, live_counts, partners,
        element_blocks, face_blocks, local_inverse, coarse_basis, coarse_inverse,
    ):
        alpha = vg_alpha.reshape(1, SLOTS)
        odd_x = lax.rem(lax.axis_index("gx"), 2)
        odd_y = lax.rem(lax.axis_index("gy"), 2)
        faces = jnp.stack([1 - odd_x, odd_x, 3 - odd_y, 2 + odd_y]).astype(jnp.int32)
        partial = pltpu.VMEM((8 * ROWS, SLOTS), F32)
        picked = pltpu.VMEM((4, NODES, SLOTS), F32)
        modal = pltpu.VMEM((MODES, SLOTS), F32)

        rows = call(restrict_kernel, "restrict", [SM, VM, VM], vec(total, SLOTS), [partial])(
            live_counts, right_side, coarse_basis
        )
        gathered = exchange(rows)
        z1, coarse, b = call(
            first_kernel, "first", [SM] + [VM] * 5,
            (vec(NODES, SLOTS), vec(SLOTS, SLOTS), vec(NODES, SLOTS)), [partial, modal],
        )(live_counts, right_side, gathered, coarse_inverse, local_inverse, coarse_basis)

        def neighbours(z):
            return [lax.ppermute(z, axes, p) for p in pairs]

        def own(z):
            return call(own_kernel, "own", [VM] * 4, vec(NODES, SLOTS), [partial])(
                z, element_blocks, pressure_head, alpha
            )

        sources = neighbours(z1)
        w1, rows = call(
            image_kernel, "image", [VM, SM, SM] + [VM] * 8,
            (vec(NODES, SLOTS), vec(total, SLOTS)), [picked, partial],
        )(own(z1), live_counts, faces, partners, *sources, face_blocks, b, coarse_basis)
        gathered = exchange(rows)
        z2, v2, sums = call(
            second_kernel, "second", [VM, VM, SM] + [VM] * 5,
            (vec(NODES, SLOTS), vec(NODES, SLOTS), vec(8, SLOTS)),
            [pltpu.VMEM((SLOTS, SLOTS), F32), partial, modal],
        )(b, w1, live_counts, coarse, gathered, coarse_inverse, local_inverse, coarse_basis)
        sources = neighbours(z2)
        rows = call(
            last_image_kernel, "last_image", [VM, SM, SM] + [VM] * 8,
            vec(total, SLOTS), [picked, partial],
        )(own(z2), live_counts, faces, partners, *sources, face_blocks, b, v2)
        gathered = exchange(rows)
        update, hess = call(
            final_kernel, "final", [VM] * 4, (vec(NODES, SLOTS), vec(2, 3)), []
        )(sums, gathered, z1, z2)
        return update, hess.T

    placed = (
        P(None, axes), P(None, axes), P(axes), P(axes), P(None, axes),
        P(None, None, axes), P(None, None, None, axes), P(None, None, axes), P(None, None, axes),
        P(axes, None),
    )
    return jax.shard_map(
        shards, mesh=mesh, in_specs=placed, out_specs=(P(None, axes), P()), check_vma=False
    )
```

time: 967 us -> 106 us (0.11)
  waiting for transfers between devices: 422 us -> 15.2 us
  blocking collectives: 382 us -> 43.1 us
  matrix products: 49.4 us -> 0 us
  local copies, waits for them, and re-layouts: 48 us -> 8.04 us
  between operations: 24.9 us -> 1.5 us
  other arithmetic: 16.8 us -> 0.08 us
    unnamed x4 -> x0, waiting for transfers between devices: 422 us -> none
    psum x5 -> x0, blocking collectives: 382 us -> none  [the longest x2 153 us: shards(): coeffs = lax.psum(jnp.stack(partials), ('gx', 'gy'))]
    dot_general x18 -> x0, matrix products: 49.4 us -> none  [the longest x12 38.6 us: apply_blocks(): jnp.einsum('ije,je->ie', blocks.astype(jnp.float32), vector_in, precision...]
    all_to_all x0 -> x2, blocking collectives: none -> 43.1 us  [exchange(): return lax.all_to_all(rows, axes, 0, 0, tiled=True)]
    squeeze x9 -> x0, local copies, waits for them, and re-layouts: 27.2 us -> none  [the longest x5 25.4 us: shards(): summed = summed + apply_blocks(face_blocks[direction], picked)]
    all_to_all x0 -> x1, starting transfers between devices: none -> 15.7 us  [exchange(): return lax.all_to_all(rows, axes, 0, 0, tiled=True)]
    all_to_all x0 -> x1, waiting for transfers between devices: none -> 13 us  [exchange(): return lax.all_to_all(rows, axes, 0, 0, tiled=True)]
  transfers between devices with their start and end apart: 10 -> 9, of which waited for: 3 -> 3; matrix products, arithmetic and copies ran while one was open for 8% -> 0% of each run, Pallas kernels for 0% -> 1%
where the time goes in v1:
time: 106 us; the launch traced here: 105 us
  blocking collectives  43.1 us (41%)
  starting transfers between devices  28.1 us (27%)
  waiting for transfers between devices  15.2 us (14%)
  Pallas kernels  9.14 us (9%)
  local copies, waits for them, and re-layouts  8.04 us (8%)
  between operations  1.5 us (1%)
    all_to_all x2, blocking collectives, exchange(): return lax.all_to_all(rows, axes, 0, 0, tiled=True)  43.1 us
    all_to_all x1, starting transfers between devices, exchange(): return lax.all_to_all(rows, axes, 0, 0, tiled=True)  15.7 us
    all_to_all x1, waiting for transfers between devices, exchange(): return lax.all_to_all(rows, axes, 0, 0, tiled=True)  13 us
    ppermute x8, starting transfers between devices, neighbours(): return [lax.ppermute(z, axes, p) for p in pairs]  12.5 us
    unnamed x30, local copies, waits for them, and re-layouts  8.04 us
    ppermute x8, waiting for transfers between devices, neighbours(): return [lax.ppermute(z, axes, p) for p in pairs]  2.17 us
  transfers between devices with their start and end apart: 9, of which 3 were waited for; matrix products, arithmetic and copies ran while one was open for 0% of the time, Pallas kernels for 1%

profile of v1, /device:TPU:1, one launch (start us, length us, event | category | flops | bytes accessed | tf_op | source)
XLA Modules:
  0.0 105.2 jit_solution(2272136843454763071)
XLA Ops:
  1.3 0.0 copy-start
  1.3 1.2 %copy-done = bf16[64,64,128]{2,1,0:T(8,128)(2,1)S(1)} copy-done((bf16[64,64,128]{2,1,0:T(8,128)(2,1)S(1)}, bf16[64,64,128]{2,1,0:T(8,128)(2,1)}, u32[]{:S(2)}) %copy-start) | copy-done | bytes 1048600
  2.5 0.8 copy-done.10
  3.3 1.1 %restrict.1 = f32[256,128]{1,0:T(8,128)} custom-call(s32[1]{0:T(128)S(6)} %copy.15.count_ref, f32[64,128]{1,0:T(8,128)S(1)} %copy-done.10, bf16[64,64,128]{2,1,0:T(8,128)(2,1)S(1)} %copy-done), custom_call_target="tpu_custom_call" | custom-call | tf_op jit(solution)/shard_map/restrict/pallas_call | solution.py:261
  4.4 15.7 %all-to-all-start = ((f32[256,1,128]{2,1,0:T(1,128)}), f32[256,1,128]{2,1,0:T(1,128)S(1)}, u32[]{:S(2)}, u32[]{:S(2)}) async-start(f32[256,1,128]{2,1,0:T(1,128)} %bitcast.1), calls=%async_computation | async-start | bytes 262144 | tf_op jit(solution)/shard_map/all_to_all | solution.py:247
  20.1 13.0 %all-to-all-done = f32[256,1,128]{2,1,0:T(1,128)S(1)} async-done(((f32[256,1,128]{2,1,0:T(1,128)}), f32[256,1,128]{2,1,0:T(1,128)S(1)}, u32[]{:S(2)}, u32[]{:S(2)}) %all-to-all-start) | async-done | bytes 131104 | tf_op jit(solution)/shard_map/all_to_all | solution.py:247
  33.1 1.2 %copy-done.1 = bf16[64,64,128]{2,1,0:T(8,128)(2,1)S(1)} copy-done((bf16[64,64,128]{2,1,0:T(8,128)(2,1)S(1)}, bf16[64,64,128]{2,1,0:T(8,128)(2,1)}, u32[]{:S(2)}) %copy-start.1) | copy-done | bytes 1048600
  34.3 1.6 %copy-done.4 = bf16[64,16384]{1,0:T(8,128)(2,1)S(1)} copy-done((bf16[64,16384]{1,0:T(8,128)(2,1)S(1)}, bf16[64,16384]{1,0:T(8,128)(2,1)}, u32[]{:S(2)}) %copy-start.4) | copy-done | bytes 2097176
  35.9 1.2 %copy-done.6 = bf16[64,64,128]{2,1,0:T(8,128)(2,1)S(1)} copy-done((bf16[64,64,128]{2,1,0:T(8,128)(2,1)S(1)}, bf16[64,64,128]{2,1,0:T(8,128)(2,1)}, u32[]{:S(2)}) %copy-start.6) | copy-done | bytes 1048600
  37.1 0.8 copy-done.11
  37.9 1.3 %first.1 = (f32[64,128]{1,0:T(8,128)S(1)}, f32[128,128]{1,0:T(8,128)S(1)}, f32[64,128]{1,0:T(8,128)S(1)}) custom-call(s32[1]{0:T(128)S(6)} %copy.15.count_ref, f32[64,128]{1,0:T(8,128)S(1)} %copy-done.11, f32[256,128]{1,0:T(8,128)S(1)} %bitcast.18, bf16[64,16384]{1,0:T(8,128)(2,1)S(1)} %copy-done.4, bf16[64,64,128]{2,1,0:T(8,128)(2,1)S(1)} %copy-done.6, ...), custom_call_target="tpu_custom_call" | custom-call | tf_op jit(solution)/shard_map/first/pallas_call | solution.py:265
  39.2 0.0 copy-start.5
  39.2 0.8 collective-permute-start.3
  40.0 2.5 %collective-permute-start.2 = (f32[64,128]{1,0:T(8,128)S(1)}, f32[64,128]{1,0:T(8,128)S(1)}, u32[]{:S(2)}, u32[]{:S(2)}) collective-permute-start(f32[64,128]{1,0:T(8,128)S(1)} %get-tuple-element.13.z_ref.z1_ref), channel_id=1, source_target_pairs={{0,1},{1,0},{2,3},{3,2},{4,5},{5,4},{6,7},{7,6},{8,9},{9,8},{10,11... | collective-permute-start | bytes 98312 | tf_op jit(solution)/shard_map/ppermute | solution.py:271
  42.5 3.0 %collective-permute-start.1 = (f32[64,128]{1,0:T(8,128)S(1)}, f32[64,128]{1,0:T(8,128)S(1)}, u32[]{:S(2)}, u32[]{:S(2)}) collective-permute-start(f32[64,128]{1,0:T(8,128)S(1)} %get-tuple-element.13.z_ref.z1_ref), channel_id=1, source_target_pairs={{8,16},{16,8},{9,17},{17,9},{10,18},{18,10},{11,19},{19,11},{12,20... | collective-permute-start | bytes 98312 | tf_op jit(solution)/shard_map/ppermute | solution.py:271
  45.5 0.1 collective-permute-start
  45.6 0.1 pad_add_fusion.faces_ref
  45.7 1.2 %copy-done.8 = bf16[64,64,128]{2,1,0:T(8,128)(2,1)S(1)} copy-done((bf16[64,64,128]{2,1,0:T(8,128)(2,1)S(1)}, bf16[64,64,128]{2,1,0:T(8,128)(2,1)}, u32[]{:S(2)}) %copy-start.8) | copy-done | bytes 1048600
  46.9 0.3 own.2.own_ref
  47.3 0.4 collective-permute-done.1.s1
  47.8 2.1 %image.1 = (f32[64,128]{1,0:T(8,128)S(1)}, f32[256,128]{1,0:T(8,128)S(1)}) custom-call(f32[64,128]{1,0:T(8,128)S(1)} %own.2.own_ref, s32[1]{0:T(128)S(6)} %copy.15.count_ref, s32[4]{0:T(128)S(1)} %pad_add_fusion.faces_ref, s32[4,128]{1,0:T(4,128)S(1)} %copy-done.13, f32[64,128]{1,0:T(8,128)S(1)} %collective-permute-done.s0, ...), custom_call_target="tpu_custom_call" | custom-call | tf_op jit(solution)/shard_map/image/pallas_call | solution.py:279
  49.8 21.6 %all_to_all.33 = f32[256,1,128]{2,1,0:T(1,128)S(1)} all-to-all(f32[256,1,128]{2,1,0:T(1,128)S(1)} %bitcast.22), channel_id=1, replica_groups=mesh['gx'=32,'gy'=8] {'gx','gy'}, dimensions={0} | all-to-all | bytes 262144 | tf_op jit(solution)/shard_map/all_to_all | solution.py:247
  71.4 1.4 %second.1 = (f32[64,128]{1,0:T(8,128)S(1)}, f32[64,128]{1,0:T(8,128)S(1)}, f32[8,128]{1,0:T(8,128)S(1)}) custom-call(f32[64,128]{1,0:T(8,128)S(1)} %get-tuple-element.12.b_ref, f32[64,128]{1,0:T(8,128)S(1)} %get-tuple-element.14.w_ref, s32[1]{0:T(128)S(6)} %copy.15.count_ref, f32[128,128]{1,0:T(8,128)S(1)} %get-tuple-element.15.coarse_ref, ...), custom_call_target="tpu_custom_call" | custom-call | tf_op jit(solution)/shard_map/second/pallas_call | solution.py:284
  72.8 0.7 collective-permute-start.7
  73.5 2.3 %collective-permute-start.6 = (f32[64,128]{1,0:T(8,128)S(1)}, f32[64,128]{1,0:T(8,128)S(1)}, u32[]{:S(2)}, u32[]{:S(2)}) collective-permute-start(f32[64,128]{1,0:T(8,128)S(1)} %get-tuple-element.18.z_ref.z2_ref), channel_id=1, source_target_pairs={{0,1},{1,0},{2,3},{3,2},{4,5},{5,4},{6,7},{7,6},{8,9},{9,8},{10,11... | collective-permute-start | bytes 98312 | tf_op jit(solution)/shard_map/ppermute | solution.py:271
  75.8 3.0 %collective-permute-start.5 = (f32[64,128]{1,0:T(8,128)S(1)}, f32[64,128]{1,0:T(8,128)S(1)}, u32[]{:S(2)}, u32[]{:S(2)}) collective-permute-start(f32[64,128]{1,0:T(8,128)S(1)} %get-tuple-element.18.z_ref.z2_ref), channel_id=1, source_target_pairs={{8,16},{16,8},{9,17},{17,9},{10,18},{18,10},{11,19},{19,11},{12,20... | collective-permute-start | bytes 98312 | tf_op jit(solution)/shard_map/ppermute | solution.py:271
  78.9 0.1 collective-permute-start.4
  79.0 0.3 own.3.own_ref
  79.4 1.7 %collective-permute-done.5.s1 = f32[64,128]{1,0:T(8,128)S(1)} collective-permute-done((f32[64,128]{1,0:T(8,128)S(1)}, f32[64,128]{1,0:T(8,128)S(1)}, u32[]{:S(2)}, u32[]{:S(2)}) %collective-permute-start.5) | collective-permute-done | bytes 32800 | tf_op jit(solution)/shard_map/ppermute | solution.py:271
  81.1 1.8 %last_image.1 = f32[256,128]{1,0:T(8,128)S(1)} custom-call(f32[64,128]{1,0:T(8,128)S(1)} %own.3.own_ref, s32[1]{0:T(128)S(6)} %copy.15.count_ref, s32[4]{0:T(128)S(1)} %pad_add_fusion.faces_ref, s32[4,128]{1,0:T(4,128)S(1)} %copy-done.13, f32[64,128]{1,0:T(8,128)S(1)} %collective-permute-done.4.s0, f32[64,128]{1,0:T(8,128)S(1)} %collective-permute-done.5.s1, ...), custom_call_target="tpu_custom_call" | custom-call | tf_op jit(solution)/shard_map/last_image/pallas_call | solution.py:290
  82.9 21.5 %all_to_all.34 = f32[256,1,128]{2,1,0:T(1,128)S(1)} all-to-all(f32[256,1,128]{2,1,0:T(1,128)S(1)} %bitcast.19), channel_id=1, replica_groups=mesh['gx'=32,'gy'=8] {'gx','gy'}, dimensions={0} | all-to-all | bytes 262144 | tf_op jit(solution)/shard_map/all_to_all | solution.py:247
  104.4 0.8 final.1
  (27 shorter events, 0.1 us)
Async XLA Ops:
  0.6 45.1 %copy-start.14 = (f32[128]{0:T(128)S(1)}, f32[128]{0:T(128)}, u32[]{:S(2)}) copy-start(f32[128]{0:T(128)} %param.12) | copy-start | bytes 1540
  1.3 1.2 %copy-start = (bf16[64,64,128]{2,1,0:T(8,128)(2,1)S(1)}, bf16[64,64,128]{2,1,0:T(8,128)(2,1)}, u32[]{:S(2)}) copy-start(bf16[64,64,128]{2,1,0:T(8,128)(2,1)} %basis_ref.7) | copy-start | bytes 3145732
  2.5 0.8 copy-start.10
  3.3 42.4 %copy-start.12 = (f32[64,128]{1,0:T(8,128)S(1)}, f32[64,128]{1,0:T(8,128)}, u32[]{:S(2)}) copy-start(f32[64,128]{1,0:T(8,128)} %pressure_ref.3) | copy-start | bytes 98308
  3.3 44.5 %copy-start.2 = (bf16[64,64,128]{2,1,0:T(8,128)(2,1)S(1)}, bf16[64,64,128]{2,1,0:T(8,128)(2,1)}, u32[]{:S(2)}) copy-start(bf16[64,64,128]{2,1,0:T(8,128)(2,1)} %basis_ref.7) | copy-start | bytes 3145732
  3.3 44.5 %copy-start.13 = (s32[4,128]{1,0:T(4,128)S(1)}, s32[4,128]{1,0:T(4,128)}, u32[]{:S(2)}) copy-start(s32[4,128]{1,0:T(4,128)} %partners_ref.3) | copy-start | bytes 6148
  4.4 28.7 %all-to-all-start = ((f32[256,1,128]{2,1,0:T(1,128)}), f32[256,1,128]{2,1,0:T(1,128)S(1)}, u32[]{:S(2)}, u32[]{:S(2)}) async-start(f32[256,1,128]{2,1,0:T(1,128)} %bitcast.1), calls=%async_computation | async-start | bytes 262144 | tf_op jit(solution)/shard_map/all_to_all | solution.py:247
  33.1 1.2 %copy-start.1 = (bf16[64,64,128]{2,1,0:T(8,128)(2,1)S(1)}, bf16[64,64,128]{2,1,0:T(8,128)(2,1)}, u32[]{:S(2)}) copy-start(bf16[64,64,128]{2,1,0:T(8,128)(2,1)} %basis_ref.7) | copy-start | bytes 3145732
  34.3 1.6 %copy-start.4 = (bf16[64,16384]{1,0:T(8,128)(2,1)S(1)}, bf16[64,16384]{1,0:T(8,128)(2,1)}, u32[]{:S(2)}) copy-start(bf16[64,16384]{1,0:T(8,128)(2,1)} %inverse_ref.3) | copy-start | bytes 6291460
  35.9 1.2 %copy-start.6 = (bf16[64,64,128]{2,1,0:T(8,128)(2,1)S(1)}, bf16[64,64,128]{2,1,0:T(8,128)(2,1)}, u32[]{:S(2)}) copy-start(bf16[64,64,128]{2,1,0:T(8,128)(2,1)} %local_ref.3) | copy-start | bytes 3145732
  37.1 0.8 copy-start.11
  37.9 9.9 %copy-start.3 = (bf16[4,64,64,128]{3,2,1,0:T(8,128)(2,1)S(1)}, bf16[4,64,64,128]{3,2,1,0:T(8,128)(2,1)}, u32[]{:S(2)}) copy-start(bf16[4,64,64,128]{3,2,1,0:T(8,128)(2,1)} %blocks_ref.7) | copy-start | bytes 12582916
  39.2 32.2 %copy-start.5 = (bf16[64,16384]{1,0:T(8,128)(2,1)S(1)}, bf16[64,16384]{1,0:T(8,128)(2,1)}, u32[]{:S(2)}) copy-start(bf16[64,16384]{1,0:T(8,128)(2,1)} %inverse_ref.3) | copy-start | bytes 6291460
  39.2 32.2 %copy-start.7 = (bf16[64,64,128]{2,1,0:T(8,128)(2,1)S(1)}, bf16[64,64,128]{2,1,0:T(8,128)(2,1)}, u32[]{:S(2)}) copy-start(bf16[64,64,128]{2,1,0:T(8,128)(2,1)} %local_ref.3) | copy-start | bytes 3145732
  39.2 8.0 %collective-permute-start.3 = (f32[64,128]{1,0:T(8,128)S(1)}, f32[64,128]{1,0:T(8,128)S(1)}, u32[]{:S(2)}, u32[]{:S(2)}) collective-permute-start(f32[64,128]{1,0:T(8,128)S(1)} %get-tuple-element.13.z_ref.z1_ref), channel_id=1, source_target_pairs={{1,2},{2,1},{3,4},{4,3},{5,6},{6,5},{9,10},{10,9},{11,12},{12,11},... | collective-permute-start | bytes 98312 | tf_op jit(solution)/shard_map/ppermute | solution.py:271
  40.0 7.2 %collective-permute-start.2 = (f32[64,128]{1,0:T(8,128)S(1)}, f32[64,128]{1,0:T(8,128)S(1)}, u32[]{:S(2)}, u32[]{:S(2)}) collective-permute-start(f32[64,128]{1,0:T(8,128)S(1)} %get-tuple-element.13.z_ref.z1_ref), channel_id=1, source_target_pairs={{0,1},{1,0},{2,3},{3,2},{4,5},{5,4},{6,7},{7,6},{8,9},{9,8},{10,11... | collective-permute-start | bytes 98312 | tf_op jit(solution)/shard_map/ppermute | solution.py:271
  42.5 5.2 %collective-permute-start.1 = (f32[64,128]{1,0:T(8,128)S(1)}, f32[64,128]{1,0:T(8,128)S(1)}, u32[]{:S(2)}, u32[]{:S(2)}) collective-permute-start(f32[64,128]{1,0:T(8,128)S(1)} %get-tuple-element.13.z_ref.z1_ref), channel_id=1, source_target_pairs={{8,16},{16,8},{9,17},{17,9},{10,18},{18,10},{11,19},{19,11},{12,20... | collective-permute-start | bytes 98312 | tf_op jit(solution)/shard_map/ppermute | solution.py:271
  45.5 2.2 %collective-permute-start = (f32[64,128]{1,0:T(8,128)S(1)}, f32[64,128]{1,0:T(8,128)S(1)}, u32[]{:S(2)}, u32[]{:S(2)}) collective-permute-start(f32[64,128]{1,0:T(8,128)S(1)} %get-tuple-element.13.z_ref.z1_ref), channel_id=1, source_target_pairs={{0,8},{8,0},{1,9},{9,1},{2,10},{10,2},{3,11},{11,3},{4,12},{12,4},... | collective-permute-start | bytes 98312 | tf_op jit(solution)/shard_map/ppermute | solution.py:271
  45.7 1.2 %copy-start.8 = (bf16[64,64,128]{2,1,0:T(8,128)(2,1)S(1)}, bf16[64,64,128]{2,1,0:T(8,128)(2,1)}, u32[]{:S(2)}) copy-start(bf16[64,64,128]{2,1,0:T(8,128)(2,1)} %blocks_ref.6) | copy-start | bytes 3145732
  47.8 31.2 %copy-start.9 = (bf16[64,64,128]{2,1,0:T(8,128)(2,1)S(1)}, bf16[64,64,128]{2,1,0:T(8,128)(2,1)}, u32[]{:S(2)}) copy-start(bf16[64,64,128]{2,1,0:T(8,128)(2,1)} %blocks_ref.6) | copy-start | bytes 3145732
  72.8 6.5 %collective-permute-start.7 = (f32[64,128]{1,0:T(8,128)S(1)}, f32[64,128]{1,0:T(8,128)S(1)}, u32[]{:S(2)}, u32[]{:S(2)}) collective-permute-start(f32[64,128]{1,0:T(8,128)S(1)} %get-tuple-element.18.z_ref.z2_ref), channel_id=1, source_target_pairs={{1,2},{2,1},{3,4},{4,3},{5,6},{6,5},{9,10},{10,9},{11,12},{12,11},... | collective-permute-start | bytes 98312 | tf_op jit(solution)/shard_map/ppermute | solution.py:271
  73.5 5.8 %collective-permute-start.6 = (f32[64,128]{1,0:T(8,128)S(1)}, f32[64,128]{1,0:T(8,128)S(1)}, u32[]{:S(2)}, u32[]{:S(2)}) collective-permute-start(f32[64,128]{1,0:T(8,128)S(1)} %get-tuple-element.18.z_ref.z2_ref), channel_id=1, source_target_pairs={{0,1},{1,0},{2,3},{3,2},{4,5},{5,4},{6,7},{7,6},{8,9},{9,8},{10,11... | collective-permute-start | bytes 98312 | tf_op jit(solution)/shard_map/ppermute | solution.py:271
  75.8 5.2 %collective-permute-start.5 = (f32[64,128]{1,0:T(8,128)S(1)}, f32[64,128]{1,0:T(8,128)S(1)}, u32[]{:S(2)}, u32[]{:S(2)}) collective-permute-start(f32[64,128]{1,0:T(8,128)S(1)} %get-tuple-element.18.z_ref.z2_ref), channel_id=1, source_target_pairs={{8,16},{16,8},{9,17},{17,9},{10,18},{18,10},{11,19},{19,11},{12,20... | collective-permute-start | bytes 98312 | tf_op jit(solution)/shard_map/ppermute | solution.py:271
  78.9 2.2 %collective-permute-start.4 = (f32[64,128]{1,0:T(8,128)S(1)}, f32[64,128]{1,0:T(8,128)S(1)}, u32[]{:S(2)}, u32[]{:S(2)}) collective-permute-start(f32[64,128]{1,0:T(8,128)S(1)} %get-tuple-element.18.z_ref.z2_ref), channel_id=1, source_target_pairs={{0,8},{8,0},{1,9},{9,1},{2,10},{10,2},{3,11},{11,3},{4,12},{12,4},... | collective-permute-start | bytes 98312 | tf_op jit(solution)/shard_map/ppermute | solution.py:271

commit v2 on v1

--- a/solution.py
+++ b/solution.py
@@ -17,6 +17,9 @@
 F32 = jnp.float32
 VM = pl.BlockSpec(memory_space=pltpu.VMEM)
 SM = pl.BlockSpec(memory_space=pltpu.SMEM)
+HB = pl.BlockSpec(memory_space=pltpu.HBM)
+PIECES = 4
+ORDER = (0, 2, 3, 1)
 
 
 def live_mask(count):
@@ -38,7 +41,7 @@
     return parts[0]
 
 
-def blocks_into(partial_ref, terms):
+def blocks_into(partial_ref, terms, first=0, last=NODES):
     def body(i, carry):
         total = None
         for block_at, vector in terms:
@@ -47,7 +50,7 @@
         partial_ref[pl.ds(pl.multiple_of(8 * i, 8), 8), :] = total
         return carry
 
-    lax.fori_loop(0, NODES, body, 0, unroll=4)
+    lax.fori_loop(first, last, body, 0, unroll=4)
 
 
 def send_row(partial_ref, out_ref):
@@ -68,11 +71,34 @@
             partial_ref[rows, :] = jnp.zeros((8, SLOTS), F32)
 
 
-def restrict_kernel(count_ref, rhs_ref, basis_ref, row_ref, partial_ref):
-    b = rhs_ref[...] * live_mask(count_ref[0])
-    blocks_into(partial_ref, [(lambda m: basis_ref[m], lambda: b)])
+def restrict_kernel(
+    count_ref, rhs_hbm, basis_hbm, local_hbm, inverse_hbm,
+    row_ref, b_ref, basis_ref, local_ref, inverse_ref,
+    partial_ref, rhs_sem, basis_sem, local_sem, inverse_sem,
+):
+    rhs_copy = pltpu.make_async_copy(rhs_hbm, b_ref, rhs_sem)
+    rhs_copy.start()
+    modes = MODES // PIECES
+    copies = []
+    for k in range(PIECES):
+        piece = pl.ds(k * modes, modes)
+        copies.append(pltpu.make_async_copy(basis_hbm.at[piece], basis_ref.at[piece], basis_sem.at[k]))
+        copies[-1].start()
+    local_copy = pltpu.make_async_copy(local_hbm, local_ref, local_sem)
+    local_copy.start()
+    inverse_copy = pltpu.make_async_copy(inverse_hbm, inverse_ref, inverse_sem)
+    inverse_copy.start()
     put_dots(partial_ref, [])
+    rhs_copy.wait()
+    b_ref[...] = b_ref[...] * live_mask(count_ref[0])
+    for k, copy in enumerate(copies):
+        copy.wait()
+        blocks_into(
+            partial_ref, [(lambda m: basis_ref[m], lambda: b_ref[...])], k * modes, (k + 1) * modes
+        )
     send_row(partial_ref, row_ref)
+    local_copy.wait()
+    inverse_copy.wait()
 
 
 def halves(rows_ref):
@@ -99,12 +125,11 @@
 
 
 def first_kernel(
-    count_ref, rhs_ref, gathered_ref, inverse_ref, local_ref, basis_ref,
-    z_ref, coarse_ref, b_ref, partial_ref, modal_ref,
+    count_ref, b_ref, gathered_ref, inverse_ref, local_ref, basis_ref,
+    z_ref, coarse_ref, partial_ref, modal_ref,
 ):
     mask = live_mask(count_ref[0])
     coarse_ref[...] = halves(gathered_ref)
-    b_ref[...] = rhs_ref[...] * mask
     z = precondition(b_ref, coarse_ref, inverse_ref, local_ref, basis_ref, partial_ref, modal_ref)
     z_ref[...] = z * mask
 
@@ -129,8 +154,28 @@
     z_ref[...] = z * mask
 
 
-def own_kernel(z_ref, blocks_ref, pressure_ref, alpha_ref, out_ref, partial_ref):
-    blocks_into(partial_ref, [(lambda i: blocks_ref[i], lambda: z_ref[...])])
+def face_of(q):
+    if q < 2:
+        odd = lax.rem(lax.axis_index("gx"), 2)
+        return 1 - odd if q == 0 else odd
+    odd = lax.rem(lax.axis_index("gy"), 2)
+    return 3 - odd if q == 2 else 2 + odd
+
+
+def pick(source_ref, partners_ref, q):
+    slots = jnp.broadcast_to(partners_ref[pl.ds(face_of(q), 1), :], (NODES, SLOTS))
+    return jnp.take_along_axis(source_ref[...], slots, axis=1)
+
+
+def own_kernel(
+    z_ref, blocks_ref, pressure_ref, alpha_ref, partners_ref, s0, faces_ref, out_ref, picked_ref, partial_ref
+):
+    picked_ref[0] = pick(s0, partners_ref, 0)
+    face = face_of(0)
+    blocks_into(
+        partial_ref,
+        [(lambda i: blocks_ref[i], lambda: z_ref[...]), (lambda i: faces_ref[face, i], lambda: picked_ref[0])],
+    )
     alpha = alpha_ref[...]
     scaled = jnp.abs(alpha * pressure_ref[...])
     power = jnp.exp((shape_exponent - 1.0) * jnp.log(scaled))
@@ -139,24 +184,22 @@
     out_ref[...] = fold_rows(partial_ref, NODES) + storage * z_ref[...]
 
 
-def faces_sum(own_ref, count_ref, faces_ref, partners_ref, source_refs, blocks_ref, picked_ref, partial_ref):
+def faces_sum(own_ref, count_ref, partners_ref, source_refs, blocks_ref, picked_ref, partial_ref):
+    terms = []
     for q, source_ref in enumerate(source_refs):
-        slots = jnp.broadcast_to(partners_ref[pl.ds(faces_ref[q], 1), :], (NODES, SLOTS))
-        picked_ref[q] = jnp.take_along_axis(source_ref[...], slots, axis=1)
-    faces = [faces_ref[q] for q in range(4)]
-    blocks_into(
-        partial_ref,
-        [(lambda i, q=q: blocks_ref[faces[q], i], lambda q=q: picked_ref[q]) for q in range(4)],
-    )
+        picked_ref[q] = pick(source_ref, partners_ref, q + 1)
+        face = face_of(q + 1)
+        terms.append((lambda i, face=face: blocks_ref[face, i], lambda q=q: picked_ref[q]))
+    blocks_into(partial_ref, terms)
     return (own_ref[...] + fold_rows(partial_ref, NODES)) * live_mask(count_ref[0])
 
 
 def image_kernel(
-    own_ref, count_ref, faces_ref, partners_ref, s0, s1, s2, s3, blocks_ref, b_ref, basis_ref,
+    own_ref, count_ref, partners_ref, s1, s2, s3, blocks_ref, b_ref, basis_ref,
     w_ref, row_ref, picked_ref, partial_ref,
 ):
     w_ref[...] = faces_sum(
-        own_ref, count_ref, faces_ref, partners_ref, (s0, s1, s2, s3), blocks_ref, picked_ref, partial_ref
+        own_ref, count_ref, partners_ref, (s1, s2, s3), blocks_ref, picked_ref, partial_ref
     )
     blocks_into(partial_ref, [(lambda m: basis_ref[m], lambda: w_ref[...])])
     w = w_ref[...]
@@ -166,11 +209,11 @@
 
 
 def last_image_kernel(
-    own_ref, count_ref, faces_ref, partners_ref, s0, s1, s2, s3, blocks_ref, b_ref, v_ref,
+    own_ref, count_ref, partners_ref, s1, s2, s3, blocks_ref, b_ref, v_ref,
     row_ref, picked_ref, partial_ref,
 ):
     w = faces_sum(
-        own_ref, count_ref, faces_ref, partners_ref, (s0, s1, s2, s3), blocks_ref, picked_ref, partial_ref
+        own_ref, count_ref, partners_ref, (s1, s2, s3), blocks_ref, picked_ref, partial_ref
     )
     b = b_ref[...]
     v = v_ref[...]
@@ -231,7 +274,7 @@
     for i in range(n_gx):
         for j in range(n_gy):
             if i + 1 < n_gx:
-                pairs[i % 2] .extend([(at(i, j), at(i + 1, j)), (at(i + 1, j), at(i, j))])
+                pairs[i % 2].extend([(at(i, j), at(i + 1, j)), (at(i + 1, j), at(i, j))])
             if j + 1 < n_gy:
                 pairs[2 + j % 2].extend([(at(i, j), at(i, j + 1)), (at(i, j + 1), at(i, j))])
     return pairs
@@ -251,46 +294,51 @@
         element_blocks, face_blocks, local_inverse, coarse_basis, coarse_inverse,
     ):
         alpha = vg_alpha.reshape(1, SLOTS)
-        odd_x = lax.rem(lax.axis_index("gx"), 2)
-        odd_y = lax.rem(lax.axis_index("gy"), 2)
-        faces = jnp.stack([1 - odd_x, odd_x, 3 - odd_y, 2 + odd_y]).astype(jnp.int32)
         partial = pltpu.VMEM((8 * ROWS, SLOTS), F32)
-        picked = pltpu.VMEM((4, NODES, SLOTS), F32)
+        picked = pltpu.VMEM((3, NODES, SLOTS), F32)
         modal = pltpu.VMEM((MODES, SLOTS), F32)
 
-        rows = call(restrict_kernel, "restrict", [SM, VM, VM], vec(total, SLOTS), [partial])(
-            live_counts, right_side, coarse_basis
-        )
+        in_hbm = lambda x: pltpu.with_memory_space_constraint(x, pltpu.HBM)
+        held = lambda x: jax.ShapeDtypeStruct(x.shape, x.dtype)
+        semaphore = pltpu.SemaphoreType.DMA
+        rows, b, basis, local, inverse = call(
+            restrict_kernel, "restrict", [SM] + [HB] * 4,
+            (vec(total, SLOTS), held(right_side), held(coarse_basis), held(local_inverse), held(coarse_inverse)),
+            [partial, semaphore, semaphore((PIECES,)), semaphore, semaphore],
+        )(live_counts, *(in_hbm(x) for x in (right_side, coarse_basis, local_inverse, coarse_inverse)))
         gathered = exchange(rows)
-        z1, coarse, b = call(
+        z1, coarse = call(
             first_kernel, "first", [SM] + [VM] * 5,
-            (vec(NODES, SLOTS), vec(SLOTS, SLOTS), vec(NODES, SLOTS)), [partial, modal],
-        )(live_counts, right_side, gathered, coarse_inverse, local_inverse, coarse_basis)
+            (vec(NODES, SLOTS), vec(SLOTS, SLOTS)), [partial, modal],
+        )(live_counts, b, gathered, inverse, local, basis)
 
         def neighbours(z):
-            return [lax.ppermute(z, axes, p) for p in pairs]
-
-        def own(z):
-            return call(own_kernel, "own", [VM] * 4, vec(NODES, SLOTS), [partial])(
-                z, element_blocks, pressure_head, alpha
+            sources = [None] * 4
+            for q in ORDER:
+                sources[q] = lax.ppermute(z, axes, pairs[q])
+            return sources
+
+        def own(z, source):
+            return call(own_kernel, "own", [VM] * 7, vec(NODES, SLOTS), [pltpu.VMEM((1, NODES, SLOTS), F32), partial])(
+                z, element_blocks, pressure_head, alpha, partners, source, face_blocks
             )
 
         sources = neighbours(z1)
         w1, rows = call(
-            image_kernel, "image", [VM, SM, SM] + [VM] * 8,
+            image_kernel, "image", [VM, SM] + [VM] * 7,
             (vec(NODES, SLOTS), vec(total, SLOTS)), [picked, partial],
-        )(own(z1), live_counts, faces, partners, *sources, face_blocks, b, coarse_basis)
+        )(own(z1, sources[0]), live_counts, partners, *sources[1:], face_blocks, b, basis)
         gathered = exchange(rows)
         z2, v2, sums = call(
             second_kernel, "second", [VM, VM, SM] + [VM] * 5,
             (vec(NODES, SLOTS), vec(NODES, SLOTS), vec(8, SLOTS)),
             [pltpu.VMEM((SLOTS, SLOTS), F32), partial, modal],
-        )(b, w1, live_counts, coarse, gathered, coarse_inverse, local_inverse, coarse_basis)
+        )(b, w1, live_counts, coarse, gathered, inverse, local, basis)
         sources = neighbours(z2)
         rows = call(
-            last_image_kernel, "last_image", [VM, SM, SM] + [VM] * 8,
+            last_image_kernel, "last_image", [VM, SM] + [VM] * 7,
             vec(total, SLOTS), [picked, partial],
-        )(own(z2), live_counts, faces, partners, *sources, face_blocks, b, v2)
+        )(own(z2, sources[0]), live_counts, partners, *sources[1:], face_blocks, b, v2)
         gathered = exchange(rows)
         update, hess = call(
             final_kernel, "final", [VM] * 4, (vec(NODES, SLOTS), vec(2, 3)), []

time: 106 us -> 98.1 us (0.925)
  blocking collectives: 43.1 us -> 70.6 us
  starting transfers between devices: 28.1 us -> 12.3 us
  waiting for transfers between devices: 15.2 us -> 3.9 us
  local copies, waits for them, and re-layouts: 8.04 us -> 0.02 us
    all_to_all x2 -> x3, blocking collectives: 43.1 us -> 70.6 us  [exchange(): return lax.all_to_all(rows, axes, 0, 0, tiled=True)]
    all_to_all x1 -> x0, starting transfers between devices: 15.7 us -> none  [exchange(): return lax.all_to_all(rows, axes, 0, 0, tiled=True)]
    all_to_all x1 -> x0, waiting for transfers between devices: 13 us -> none  [exchange(): return lax.all_to_all(rows, axes, 0, 0, tiled=True)]
    unnamed x30 -> x10, local copies, waits for them, and re-layouts: 8.04 us -> 0.02 us
    ppermute x8, waiting for transfers between devices: 2.17 us -> 3.9 us  [neighbours(): sources[q] = lax.ppermute(z, axes, pairs[q])]
  transfers between devices with their start and end apart: 9 -> 8, of which waited for: 3 -> 2; matrix products, arithmetic and copies ran while one was open for 0% -> 0% of each run, Pallas kernels for 1% -> 1%
where the time goes in v2:
time: 98.1 us; the launch traced here: 97.8 us
  blocking collectives  70.6 us (72%)
  starting transfers between devices  12.3 us (13%)
  Pallas kernels  9.59 us (10%)
  waiting for transfers between devices  3.9 us (4%)
  between operations  1.46 us (1%)
    all_to_all x3, blocking collectives, exchange(): return lax.all_to_all(rows, axes, 0, 0, tiled=True)  70.6 us
    ppermute x8, starting transfers between devices, neighbours(): sources[q] = lax.ppermute(z, axes, pairs[q])  12.3 us
    ppermute x8, waiting for transfers between devices, neighbours(): sources[q] = lax.ppermute(z, axes, pairs[q])  3.9 us
    pallas_call x1, Pallas kernels, shards(): call(restrict_kernel, 'restrict', [SM] + [HB] * 4, (vec(total, SLOTS), he...  2.39 us
  transfers between devices with their start and end apart: 8, of which 2 were waited for; matrix products, arithmetic and copies ran while one was open for 0% of the time, Pallas kernels for 1%

profile of v2, /device:TPU:1, one launch (start us, length us, event | category | flops | bytes accessed | tf_op | source)
XLA Modules:
  0.0 97.8 jit_solution(10575463120513539559)
XLA Ops:
  1.3 0.0 copy-start.1
  1.3 2.4 %restrict.1 = (f32[256,128]{1,0:T(8,128)S(1)}, f32[64,128]{1,0:T(8,128)S(1)}, bf16[64,64,128]{2,1,0:T(8,128)(2,1)S(1)}, bf16[64,64,128]{2,1,0:T(8,128)(2,1)S(1)}, bf16[64,16384]{1,0:T(8,128)(2,1)S(1)}) custom-call(s32[1]{0:T(128)S(6)} %copy.15.count_ref, f32[64,128]{1,0:T(8,128)} %rhs_hbm.1, bf16[64,64,128]{2,1,0:T(8,128)(2,1)} %basis_hbm.1, ...), custom_call_target="tpu_custom_call" | custom-call | tf_op jit(solution)/shard_map/restrict/pallas_call | solution.py:304
  3.7 28.5 %all_to_all.33 = f32[256,1,128]{2,1,0:T(1,128)S(1)} all-to-all(f32[256,1,128]{2,1,0:T(1,128)S(1)} %bitcast.19), channel_id=1, replica_groups=mesh['gx'=32,'gy'=8] {'gx','gy'}, dimensions={0} | all-to-all | bytes 262144 | tf_op jit(solution)/shard_map/all_to_all | solution.py:290
  32.2 1.4 %first.1 = (f32[64,128]{1,0:T(8,128)S(1)}, f32[128,128]{1,0:T(8,128)S(1)}) custom-call(s32[1]{0:T(128)S(6)} %copy.15.count_ref, f32[64,128]{1,0:T(8,128)S(1)} %get-tuple-element.16.b_ref, f32[256,128]{1,0:T(8,128)S(1)} %bitcast.16, bf16[64,16384]{1,0:T(8,128)(2,1)S(1)} %get-tuple-element.18.inverse_ref, ...), custom_call_target="tpu_custom_call" | custom-call | tf_op jit(solution)/shard_map/first/pallas_call | solution.py:310
  33.6 0.7 collective-permute-start
  34.2 0.7 collective-permute-start.3
  34.9 2.2 %collective-permute-start.2 = (f32[64,128]{1,0:T(8,128)S(1)}, f32[64,128]{1,0:T(8,128)S(1)}, u32[]{:S(2)}, u32[]{:S(2)}) collective-permute-start(f32[64,128]{1,0:T(8,128)S(1)} %get-tuple-element.21.z_ref.z1_ref), channel_id=1, source_target_pairs={{0,1},{1,0},{2,3},{3,2},{4,5},{5,4},{6,7},{7,6},{8,9},{9,8},{10,11... | collective-permute-start | bytes 98312 | tf_op jit(solution)/shard_map/ppermute | solution.py:318
  37.1 2.6 %collective-permute-start.1 = (f32[64,128]{1,0:T(8,128)S(1)}, f32[64,128]{1,0:T(8,128)S(1)}, u32[]{:S(2)}, u32[]{:S(2)}) collective-permute-start(f32[64,128]{1,0:T(8,128)S(1)} %get-tuple-element.21.z_ref.z1_ref), channel_id=1, source_target_pairs={{8,16},{16,8},{9,17},{17,9},{10,18},{18,10},{11,19},{19,11},{12,20... | collective-permute-start | bytes 98312 | tf_op jit(solution)/shard_map/ppermute | solution.py:318
  39.7 0.0 collective-permute-done.s0
  39.7 0.0 copy-done.1
  39.7 0.0 copy-done
  39.7 0.0 copy-done.2
  39.7 0.0 copy-done.3
  39.8 0.7 own.2.own_ref
  40.4 0.0 collective-permute-done.3.s3
  40.4 0.0 collective-permute-done.2.s2
  40.4 1.9 %collective-permute-done.1.s1 = f32[64,128]{1,0:T(8,128)S(1)} collective-permute-done((f32[64,128]{1,0:T(8,128)S(1)}, f32[64,128]{1,0:T(8,128)S(1)}, u32[]{:S(2)}, u32[]{:S(2)}) %collective-permute-start.1) | collective-permute-done | bytes 32800 | tf_op jit(solution)/shard_map/ppermute | solution.py:318
  42.4 1.3 %image.1 = (f32[64,128]{1,0:T(8,128)S(1)}, f32[256,128]{1,0:T(8,128)S(1)}) custom-call(f32[64,128]{1,0:T(8,128)S(1)} %own.2.own_ref, s32[1]{0:T(128)S(6)} %copy.15.count_ref, s32[4,128]{1,0:T(4,128)S(1)} %copy-done.3, f32[64,128]{1,0:T(8,128)S(1)} %collective-permute-done.1.s1, f32[64,128]{1,0:T(8,128)S(1)} %collective-permute-done.2.s2, ...), custom_call_target="tpu_custom_call" | custom-call | tf_op jit(solution)/shard_map/image/pallas_call | solution.py:327
  43.7 21.0 %all_to_all.34 = f32[256,1,128]{2,1,0:T(1,128)S(1)} all-to-all(f32[256,1,128]{2,1,0:T(1,128)S(1)} %bitcast.18), channel_id=1, replica_groups=mesh['gx'=32,'gy'=8] {'gx','gy'}, dimensions={0} | all-to-all | bytes 262144 | tf_op jit(solution)/shard_map/all_to_all | solution.py:290
  64.7 1.4 %second.1 = (f32[64,128]{1,0:T(8,128)S(1)}, f32[64,128]{1,0:T(8,128)S(1)}, f32[8,128]{1,0:T(8,128)S(1)}) custom-call(f32[64,128]{1,0:T(8,128)S(1)} %get-tuple-element.16.b_ref, f32[64,128]{1,0:T(8,128)S(1)} %get-tuple-element.22.w_ref, s32[1]{0:T(128)S(6)} %copy.15.count_ref, f32[128,128]{1,0:T(8,128)S(1)} %get-tuple-element.23.coarse_ref, ...), custom_call_target="tpu_custom_call" | custom-call | tf_op jit(solution)/shard_map/second/pallas_call | solution.py:332
  66.1 0.7 collective-permute-start.4
  66.8 0.7 collective-permute-start.7
  67.5 2.2 %collective-permute-start.6 = (f32[64,128]{1,0:T(8,128)S(1)}, f32[64,128]{1,0:T(8,128)S(1)}, u32[]{:S(2)}, u32[]{:S(2)}) collective-permute-start(f32[64,128]{1,0:T(8,128)S(1)} %get-tuple-element.26.z_ref.z2_ref), channel_id=1, source_target_pairs={{0,1},{1,0},{2,3},{3,2},{4,5},{5,4},{6,7},{7,6},{8,9},{9,8},{10,11... | collective-permute-start | bytes 98312 | tf_op jit(solution)/shard_map/ppermute | solution.py:318
  69.7 2.6 %collective-permute-start.5 = (f32[64,128]{1,0:T(8,128)S(1)}, f32[64,128]{1,0:T(8,128)S(1)}, u32[]{:S(2)}, u32[]{:S(2)}) collective-permute-start(f32[64,128]{1,0:T(8,128)S(1)} %get-tuple-element.26.z_ref.z2_ref), channel_id=1, source_target_pairs={{8,16},{16,8},{9,17},{17,9},{10,18},{18,10},{11,19},{19,11},{12,20... | collective-permute-start | bytes 98312 | tf_op jit(solution)/shard_map/ppermute | solution.py:318
  72.3 0.0 collective-permute-done.4.s0
  72.3 0.7 own.3.own_ref
  72.9 0.0 collective-permute-done.7.s3
  73.0 0.0 collective-permute-done.6.s2
  73.0 2.0 %collective-permute-done.5.s1 = f32[64,128]{1,0:T(8,128)S(1)} collective-permute-done((f32[64,128]{1,0:T(8,128)S(1)}, f32[64,128]{1,0:T(8,128)S(1)}, u32[]{:S(2)}, u32[]{:S(2)}) %collective-permute-start.5) | collective-permute-done | bytes 32800 | tf_op jit(solution)/shard_map/ppermute | solution.py:318
  74.9 1.1 %last_image.1 = f32[256,128]{1,0:T(8,128)S(1)} custom-call(f32[64,128]{1,0:T(8,128)S(1)} %own.3.own_ref, s32[1]{0:T(128)S(6)} %copy.15.count_ref, s32[4,128]{1,0:T(4,128)S(1)} %copy-done.3, f32[64,128]{1,0:T(8,128)S(1)} %collective-permute-done.5.s1, f32[64,128]{1,0:T(8,128)S(1)} %collective-permute-done.6.s2, f32[64,128]{1,0:T(8,128)S(1)} %collective-permute-done.7.s3, ...), custom_call_target="tpu_custom_call" | custom-call | tf_op jit(solution)/shard_map/last_image/pallas_call | solution.py:338
  76.0 21.0 %all_to_all.35 = f32[256,1,128]{2,1,0:T(1,128)S(1)} all-to-all(f32[256,1,128]{2,1,0:T(1,128)S(1)} %bitcast.15), channel_id=1, replica_groups=mesh['gx'=32,'gy'=8] {'gx','gy'}, dimensions={0} | all-to-all | bytes 262144 | tf_op jit(solution)/shard_map/all_to_all | solution.py:290
  97.0 0.8 final.1
  (5 shorter events, 0.0 us)
Async XLA Ops:
  1.3 38.4 %copy-start.1 = (bf16[64,64,128]{2,1,0:T(8,128)(2,1)S(1)}, bf16[64,64,128]{2,1,0:T(8,128)(2,1)}, u32[]{:S(2)}) copy-start(bf16[64,64,128]{2,1,0:T(8,128)(2,1)} %blocks_ref.6) | copy-start | bytes 3145732
  32.2 7.5 %copy-start = (bf16[4,64,64,128]{3,2,1,0:T(8,128)(2,1)S(1)}, bf16[4,64,64,128]{3,2,1,0:T(8,128)(2,1)}, u32[]{:S(2)}) copy-start(bf16[4,64,64,128]{3,2,1,0:T(8,128)(2,1)} %blocks_ref.7) | copy-start | bytes 12582916
  32.2 7.5 %copy-start.2 = (f32[64,128]{1,0:T(8,128)S(1)}, f32[64,128]{1,0:T(8,128)}, u32[]{:S(2)}) copy-start(f32[64,128]{1,0:T(8,128)} %pressure_ref.3) | copy-start | bytes 98308
  32.2 7.6 %copy-start.3 = (s32[4,128]{1,0:T(4,128)S(1)}, s32[4,128]{1,0:T(4,128)}, u32[]{:S(2)}) copy-start(s32[4,128]{1,0:T(4,128)} %partners_ref.7) | copy-start | bytes 6148
  32.2 7.6 %copy-start.4 = (f32[128]{0:T(128)S(1)}, f32[128]{0:T(128)}, u32[]{:S(2)}) copy-start(f32[128]{0:T(128)} %param.12) | copy-start | bytes 1540
  33.6 6.1 %collective-permute-start = (f32[64,128]{1,0:T(8,128)S(1)}, f32[64,128]{1,0:T(8,128)S(1)}, u32[]{:S(2)}, u32[]{:S(2)}) collective-permute-start(f32[64,128]{1,0:T(8,128)S(1)} %get-tuple-element.21.z_ref.z1_ref), channel_id=1, source_target_pairs={{0,8},{8,0},{1,9},{9,1},{2,10},{10,2},{3,11},{11,3},{4,12},{12,4},... | collective-permute-start | bytes 98312 | tf_op jit(solution)/shard_map/ppermute | solution.py:318
  34.2 6.2 %collective-permute-start.3 = (f32[64,128]{1,0:T(8,128)S(1)}, f32[64,128]{1,0:T(8,128)S(1)}, u32[]{:S(2)}, u32[]{:S(2)}) collective-permute-start(f32[64,128]{1,0:T(8,128)S(1)} %get-tuple-element.21.z_ref.z1_ref), channel_id=1, source_target_pairs={{1,2},{2,1},{3,4},{4,3},{5,6},{6,5},{9,10},{10,9},{11,12},{12,11},... | collective-permute-start | bytes 98312 | tf_op jit(solution)/shard_map/ppermute | solution.py:318
  34.9 5.5 %collective-permute-start.2 = (f32[64,128]{1,0:T(8,128)S(1)}, f32[64,128]{1,0:T(8,128)S(1)}, u32[]{:S(2)}, u32[]{:S(2)}) collective-permute-start(f32[64,128]{1,0:T(8,128)S(1)} %get-tuple-element.21.z_ref.z1_ref), channel_id=1, source_target_pairs={{0,1},{1,0},{2,3},{3,2},{4,5},{5,4},{6,7},{7,6},{8,9},{9,8},{10,11... | collective-permute-start | bytes 98312 | tf_op jit(solution)/shard_map/ppermute | solution.py:318
  37.1 5.2 %collective-permute-start.1 = (f32[64,128]{1,0:T(8,128)S(1)}, f32[64,128]{1,0:T(8,128)S(1)}, u32[]{:S(2)}, u32[]{:S(2)}) collective-permute-start(f32[64,128]{1,0:T(8,128)S(1)} %get-tuple-element.21.z_ref.z1_ref), channel_id=1, source_target_pairs={{8,16},{16,8},{9,17},{17,9},{10,18},{18,10},{11,19},{19,11},{12,20... | collective-permute-start | bytes 98312 | tf_op jit(solution)/shard_map/ppermute | solution.py:318
  66.1 6.1 %collective-permute-start.4 = (f32[64,128]{1,0:T(8,128)S(1)}, f32[64,128]{1,0:T(8,128)S(1)}, u32[]{:S(2)}, u32[]{:S(2)}) collective-permute-start(f32[64,128]{1,0:T(8,128)S(1)} %get-tuple-element.26.z_ref.z2_ref), channel_id=1, source_target_pairs={{0,8},{8,0},{1,9},{9,1},{2,10},{10,2},{3,11},{11,3},{4,12},{12,4},... | collective-permute-start | bytes 98312 | tf_op jit(solution)/shard_map/ppermute | solution.py:318
  66.8 6.1 %collective-permute-start.7 = (f32[64,128]{1,0:T(8,128)S(1)}, f32[64,128]{1,0:T(8,128)S(1)}, u32[]{:S(2)}, u32[]{:S(2)}) collective-permute-start(f32[64,128]{1,0:T(8,128)S(1)} %get-tuple-element.26.z_ref.z2_ref), channel_id=1, source_target_pairs={{1,2},{2,1},{3,4},{4,3},{5,6},{6,5},{9,10},{10,9},{11,12},{12,11},... | collective-permute-start | bytes 98312 | tf_op jit(solution)/shard_map/ppermute | solution.py:318
  67.5 5.5 %collective-permute-start.6 = (f32[64,128]{1,0:T(8,128)S(1)}, f32[64,128]{1,0:T(8,128)S(1)}, u32[]{:S(2)}, u32[]{:S(2)}) collective-permute-start(f32[64,128]{1,0:T(8,128)S(1)} %get-tuple-element.26.z_ref.z2_ref), channel_id=1, source_target_pairs={{0,1},{1,0},{2,3},{3,2},{4,5},{5,4},{6,7},{7,6},{8,9},{9,8},{10,11... | collective-permute-start | bytes 98312 | tf_op jit(solution)/shard_map/ppermute | solution.py:318
  69.7 5.2 %collective-permute-start.5 = (f32[64,128]{1,0:T(8,128)S(1)}, f32[64,128]{1,0:T(8,128)S(1)}, u32[]{:S(2)}, u32[]{:S(2)}) collective-permute-start(f32[64,128]{1,0:T(8,128)S(1)} %get-tuple-element.26.z_ref.z2_ref), channel_id=1, source_target_pairs={{8,16},{16,8},{9,17},{17,9},{10,18},{18,10},{11,19},{19,11},{12,20... | collective-permute-start | bytes 98312 | tf_op jit(solution)/shard_map/ppermute | solution.py:318

commit v3 on v2

--- a/solution.py
+++ b/solution.py
@@ -16,14 +16,15 @@
 ROWS = MODES + DOTS
 F32 = jnp.float32
 VM = pl.BlockSpec(memory_space=pltpu.VMEM)
-SM = pl.BlockSpec(memory_space=pltpu.SMEM)
 HB = pl.BlockSpec(memory_space=pltpu.HBM)
 PIECES = 4
-ORDER = (0, 2, 3, 1)
+UNROLL = 8
+EARLY = (2, 1, 0)
+LATER = (3,)
 
 
 def live_mask(count):
-    slots = lax.broadcasted_iota(jnp.int32, (1, SLOTS), 1)
+    slots = lax.broadcasted_iota(jnp.int32, (8, SLOTS), 1)
     return (slots < count).astype(F32)
 
 
@@ -50,7 +51,7 @@
         partial_ref[pl.ds(pl.multiple_of(8 * i, 8), 8), :] = total
         return carry
 
-    lax.fori_loop(first, last, body, 0, unroll=4)
+    lax.fori_loop(first, last, body, 0, unroll=UNROLL)
 
 
 def send_row(partial_ref, out_ref):
@@ -73,7 +74,7 @@
 
 def restrict_kernel(
     count_ref, rhs_hbm, basis_hbm, local_hbm, inverse_hbm,
-    row_ref, b_ref, basis_ref, local_ref, inverse_ref,
+    row_ref, b_ref, mask_ref, basis_ref, local_ref, inverse_ref,
     partial_ref, rhs_sem, basis_sem, local_sem, inverse_sem,
 ):
     rhs_copy = pltpu.make_async_copy(rhs_hbm, b_ref, rhs_sem)
@@ -89,8 +90,9 @@
     inverse_copy = pltpu.make_async_copy(inverse_hbm, inverse_ref, inverse_sem)
     inverse_copy.start()
     put_dots(partial_ref, [])
+    mask_ref[...] = live_mask(count_ref[0])
     rhs_copy.wait()
-    b_ref[...] = b_ref[...] * live_mask(count_ref[0])
+    b_ref[...] = b_ref[...] * mask_ref[0:1, :]
     for k, copy in enumerate(copies):
         copy.wait()
         blocks_into(
@@ -113,25 +115,24 @@
         column = inverse_ref[:, pl.ds(pl.multiple_of(t * SLOTS, SLOTS), SLOTS)].astype(F32)
         return acc + column * coarse_ref[pl.ds(t, 1), :]
 
-    acc = lax.fori_loop(0, 2 * MODES, coarse_step, jnp.zeros((MODES, SLOTS), F32), unroll=8)
+    acc = lax.fori_loop(0, 2 * MODES, coarse_step, jnp.zeros((MODES, SLOTS), F32), unroll=2 * UNROLL)
     modal_ref[...] = jnp.broadcast_to(jnp.sum(acc, axis=1, keepdims=True), (MODES, SLOTS))
     blocks_into(partial_ref, [(lambda i: local_ref[i], lambda: v_ref[...])])
 
     def prolong_step(m, total):
         return total + basis_ref[m].astype(F32) * modal_ref[pl.ds(m, 1), :]
 
-    total = lax.fori_loop(0, MODES, prolong_step, jnp.zeros((NODES, SLOTS), F32), unroll=8)
+    total = lax.fori_loop(0, MODES, prolong_step, jnp.zeros((NODES, SLOTS), F32), unroll=2 * UNROLL)
     return total + fold_rows(partial_ref, NODES)
 
 
 def first_kernel(
-    count_ref, b_ref, gathered_ref, inverse_ref, local_ref, basis_ref,
+    mask_ref, b_ref, gathered_ref, inverse_ref, local_ref, basis_ref,
     z_ref, coarse_ref, partial_ref, modal_ref,
 ):
-    mask = live_mask(count_ref[0])
     coarse_ref[...] = halves(gathered_ref)
     z = precondition(b_ref, coarse_ref, inverse_ref, local_ref, basis_ref, partial_ref, modal_ref)
-    z_ref[...] = z * mask
+    z_ref[...] = z * mask_ref[0:1, :]
 
 
 def lane_of(row, k):
@@ -140,10 +141,9 @@
 
 
 def second_kernel(
-    b_ref, w_ref, count_ref, coarse_ref, gathered_ref, inverse_ref, local_ref, basis_ref,
+    b_ref, w_ref, mask_ref, coarse_ref, gathered_ref, inverse_ref, local_ref, basis_ref,
     z_ref, v_ref, sums_ref, mixed_ref, partial_ref, modal_ref,
 ):
-    mask = live_mask(count_ref[0])
     sums = jnp.sum(gathered_ref[...], axis=0, keepdims=True)
     sums_ref[...] = jnp.broadcast_to(sums, sums_ref.shape)
     along = lane_of(sums, MODES) / lane_of(sums, MODES + 2)
@@ -151,7 +151,7 @@
     mixed_ref[...] = (halves(gathered_ref) - along * coarse_ref[...]) * scale
     v_ref[...] = (w_ref[...] - along * b_ref[...]) * scale
     z = precondition(v_ref, mixed_ref, inverse_ref, local_ref, basis_ref, partial_ref, modal_ref)
-    z_ref[...] = z * mask
+    z_ref[...] = z * mask_ref[0:1, :]
 
 
 def face_of(q):
@@ -167,15 +167,20 @@
     return jnp.take_along_axis(source_ref[...], slots, axis=1)
 
 
+def face_terms(qs, source_refs, partners_ref, faces_ref, picked_ref):
+    terms = []
+    for k, (q, source_ref) in enumerate(zip(qs, source_refs)):
+        picked_ref[k] = pick(source_ref, partners_ref, q)
+        face = face_of(q)
+        terms.append((lambda i, face=face: faces_ref[face, i], lambda k=k: picked_ref[k]))
+    return terms
+
+
 def own_kernel(
-    z_ref, blocks_ref, pressure_ref, alpha_ref, partners_ref, s0, faces_ref, out_ref, picked_ref, partial_ref
-):
-    picked_ref[0] = pick(s0, partners_ref, 0)
-    face = face_of(0)
-    blocks_into(
-        partial_ref,
-        [(lambda i: blocks_ref[i], lambda: z_ref[...]), (lambda i: faces_ref[face, i], lambda: picked_ref[0])],
-    )
+    z_ref, blocks_ref, pressure_ref, alpha_ref, partners_ref, s0, s1, s2, faces_ref, out_ref, picked_ref, partial_ref
+):
+    terms = face_terms(EARLY, (s0, s1, s2), partners_ref, faces_ref, picked_ref)
+    blocks_into(partial_ref, [(lambda i: blocks_ref[i], lambda: z_ref[...])] + terms)
     alpha = alpha_ref[...]
     scaled = jnp.abs(alpha * pressure_ref[...])
     power = jnp.exp((shape_exponent - 1.0) * jnp.log(scaled))
@@ -184,23 +189,16 @@
     out_ref[...] = fold_rows(partial_ref, NODES) + storage * z_ref[...]
 
 
-def faces_sum(own_ref, count_ref, partners_ref, source_refs, blocks_ref, picked_ref, partial_ref):
-    terms = []
-    for q, source_ref in enumerate(source_refs):
-        picked_ref[q] = pick(source_ref, partners_ref, q + 1)
-        face = face_of(q + 1)
-        terms.append((lambda i, face=face: blocks_ref[face, i], lambda q=q: picked_ref[q]))
-    blocks_into(partial_ref, terms)
-    return (own_ref[...] + fold_rows(partial_ref, NODES)) * live_mask(count_ref[0])
+def all_blocks(own_ref, mask_ref, partners_ref, source_ref, faces_ref, picked_ref, partial_ref):
+    blocks_into(partial_ref, face_terms(LATER, (source_ref,), partners_ref, faces_ref, picked_ref))
+    return (own_ref[...] + fold_rows(partial_ref, NODES)) * mask_ref[0:1, :]
 
 
 def image_kernel(
-    own_ref, count_ref, partners_ref, s1, s2, s3, blocks_ref, b_ref, basis_ref,
+    own_ref, mask_ref, partners_ref, s3, blocks_ref, b_ref, basis_ref,
     w_ref, row_ref, picked_ref, partial_ref,
 ):
-    w_ref[...] = faces_sum(
-        own_ref, count_ref, partners_ref, (s1, s2, s3), blocks_ref, picked_ref, partial_ref
-    )
+    w_ref[...] = all_blocks(own_ref, mask_ref, partners_ref, s3, blocks_ref, picked_ref, partial_ref)
     blocks_into(partial_ref, [(lambda m: basis_ref[m], lambda: w_ref[...])])
     w = w_ref[...]
     b = b_ref[...]
@@ -209,12 +207,10 @@
 
 
 def last_image_kernel(
-    own_ref, count_ref, partners_ref, s1, s2, s3, blocks_ref, b_ref, v_ref,
+    own_ref, mask_ref, partners_ref, s3, blocks_ref, b_ref, v_ref,
     row_ref, picked_ref, partial_ref,
 ):
-    w = faces_sum(
-        own_ref, count_ref, partners_ref, (s1, s2, s3), blocks_ref, picked_ref, partial_ref
-    )
+    w = all_blocks(own_ref, mask_ref, partners_ref, s3, blocks_ref, picked_ref, partial_ref)
     b = b_ref[...]
     v = v_ref[...]
     partial_ref[pl.ds(0, 8 * MODES), :] = jnp.zeros((8 * MODES, SLOTS), F32)
@@ -301,44 +297,41 @@
         in_hbm = lambda x: pltpu.with_memory_space_constraint(x, pltpu.HBM)
         held = lambda x: jax.ShapeDtypeStruct(x.shape, x.dtype)
         semaphore = pltpu.SemaphoreType.DMA
-        rows, b, basis, local, inverse = call(
-            restrict_kernel, "restrict", [SM] + [HB] * 4,
-            (vec(total, SLOTS), held(right_side), held(coarse_basis), held(local_inverse), held(coarse_inverse)),
+        rows, b, mask, basis, local, inverse = call(
+            restrict_kernel, "restrict", [pl.BlockSpec(memory_space=pltpu.SMEM)] + [HB] * 4,
+            (vec(total, SLOTS), held(right_side), vec(8, SLOTS), held(coarse_basis), held(local_inverse), held(coarse_inverse)),
             [partial, semaphore, semaphore((PIECES,)), semaphore, semaphore],
         )(live_counts, *(in_hbm(x) for x in (right_side, coarse_basis, local_inverse, coarse_inverse)))
         gathered = exchange(rows)
         z1, coarse = call(
-            first_kernel, "first", [SM] + [VM] * 5,
+            first_kernel, "first", [VM] * 6,
             (vec(NODES, SLOTS), vec(SLOTS, SLOTS)), [partial, modal],
-        )(live_counts, b, gathered, inverse, local, basis)
+        )(mask, b, gathered, inverse, local, basis)
 
         def neighbours(z):
-            sources = [None] * 4
-            for q in ORDER:
-                sources[q] = lax.ppermute(z, axes, pairs[q])
-            return sources
-
-        def own(z, source):
-            return call(own_kernel, "own", [VM] * 7, vec(NODES, SLOTS), [pltpu.VMEM((1, NODES, SLOTS), F32), partial])(
-                z, element_blocks, pressure_head, alpha, partners, source, face_blocks
+            return [lax.ppermute(z, axes, pairs[q]) for q in EARLY + LATER]
+
+        def own(z, sources):
+            return call(own_kernel, "own", [VM] * 9, vec(NODES, SLOTS), [picked, partial])(
+                z, element_blocks, pressure_head, alpha, partners, *sources, face_blocks
             )
 
         sources = neighbours(z1)
         w1, rows = call(
-            image_kernel, "image", [VM, SM] + [VM] * 7,
+            image_kernel, "image", [VM] * 7,
             (vec(NODES, SLOTS), vec(total, SLOTS)), [picked, partial],
-        )(own(z1, sources[0]), live_counts, partners, *sources[1:], face_blocks, b, basis)
+        )(own(z1, sources[:3]), mask, partners, sources[3], face_blocks, b, basis)
         gathered = exchange(rows)
         z2, v2, sums = call(
-            second_kernel, "second", [VM, VM, SM] + [VM] * 5,
+            second_kernel, "second", [VM] * 8,
             (vec(NODES, SLOTS), vec(NODES, SLOTS), vec(8, SLOTS)),
             [pltpu.VMEM((SLOTS, SLOTS), F32), partial, modal],
-        )(b, w1, live_counts, coarse, gathered, inverse, local, basis)
+        )(b, w1, mask, coarse, gathered, inverse, local, basis)
         sources = neighbours(z2)
         rows = call(
-            last_image_kernel, "last_image", [VM, SM] + [VM] * 7,
+            last_image_kernel, "last_image", [VM] * 7,
             vec(total, SLOTS), [picked, partial],
-        )(own(z2, sources[0]), live_counts, partners, *sources[1:], face_blocks, b, v2)
+        )(own(z2, sources[:3]), mask, partners, sources[3], face_blocks, b, v2)
         gathered = exchange(rows)
         update, hess = call(
             final_kernel, "final", [VM] * 4, (vec(NODES, SLOTS), vec(2, 3)), []

time: 98.1 us -> 95.9 us (0.978)
  starting transfers between devices: 12.3 us -> 8.63 us
  blocking collectives: 70.6 us -> 73.3 us
    ppermute x8, starting transfers between devices: 12.3 us -> 8.63 us  [neighbours(): return [lax.ppermute(z, axes, pairs[q]) for q in EARLY + LATER]]
    all_to_all x3, blocking collectives: 70.6 us -> 73.3 us  [exchange(): return lax.all_to_all(rows, axes, 0, 0, tiled=True)]
  transfers between devices with their start and end apart: 8 -> 8, of which waited for: 2 -> 2; matrix products, arithmetic and copies ran while one was open for 0% -> 0% of each run, Pallas kernels for 1% -> 2%
where the time goes in v3:
time: 95.9 us; the launch traced here: 95.6 us
  blocking collectives  73.3 us (76%)
  Pallas kernels  9.1 us (9%)
  starting transfers between devices  8.63 us (9%)
  waiting for transfers between devices  3.13 us (3%)
  between operations  1.42 us (1%)
    all_to_all x3, blocking collectives, exchange(): return lax.all_to_all(rows, axes, 0, 0, tiled=True)  73.3 us
    ppermute x8, starting transfers between devices, neighbours(): return [lax.ppermute(z, axes, pairs[q]) for q in EARLY + LATER]  8.63 us
    ppermute x8, waiting for transfers between devices, neighbours(): return [lax.ppermute(z, axes, pairs[q]) for q in EARLY + LATER]  3.13 us
    pallas_call x1, Pallas kernels, shards(): call(restrict_kernel, 'restrict', [pl.BlockSpec(memory_space=pltpu.SMEM)]...  2.39 us
    pallas_call x2, Pallas kernels, own(): call(own_kernel, 'own', [VM] * 9, vec(NODES, SLOTS), [picked, partial])  2.09 us
  transfers between devices with their start and end apart: 8, of which 2 were waited for; matrix products, arithmetic and copies ran while one was open for 0% of the time, Pallas kernels for 2%

profile of v3, /device:TPU:1, one launch (start us, length us, event | category | flops | bytes accessed | tf_op | source)
XLA Modules:
  0.0 95.6 jit_solution(6156066109270397302)
XLA Ops:
  1.3 0.0 copy-start.1
  1.3 2.4 %restrict.1 = (f32[256,128]{1,0:T(8,128)S(1)}, f32[64,128]{1,0:T(8,128)S(1)}, f32[8,128]{1,0:T(8,128)S(1)}, bf16[64,64,128]{2,1,0:T(8,128)(2,1)S(1)}, bf16[64,64...) custom-call(s32[1]{0:T(128)S(6)} %copy.15.count_ref, f32[64,128]{1,0:T(8,128)} %rhs_hbm.1, ...), custom_call_target="tpu_custom_call" | custom-call | tf_op jit(solution)/shard_map/restrict/pallas_call | solution.py:300
  3.7 28.5 %all_to_all.33 = f32[256,1,128]{2,1,0:T(1,128)S(1)} all-to-all(f32[256,1,128]{2,1,0:T(1,128)S(1)} %bitcast.18), channel_id=1, replica_groups=mesh['gx'=32,'gy'=8] {'gx','gy'}, dimensions={0} | all-to-all | bytes 262144 | tf_op jit(solution)/shard_map/all_to_all | solution.py:286
  32.2 1.2 %first.1 = (f32[64,128]{1,0:T(8,128)S(1)}, f32[128,128]{1,0:T(8,128)S(1)}) custom-call(f32[8,128]{1,0:T(8,128)S(1)} %get-tuple-element.18.mask_ref, f32[64,128]{1,0:T(8,128)S(1)} %get-tuple-element.17.b_ref, f32[256,128]{1,0:T(8,128)S(1)} %bitcast.16, bf16[64,16384]{1,0:T(8,128)(2,1)S(1)} %get-tuple-element.20.inverse_ref, ...), custom_call_target="tpu_custom_call" | custom-call | tf_op jit(solution)/shard_map/first/pallas_call | solution.py:306
  33.4 0.7 collective-permute-start.2
  34.1 2.1 %collective-permute-start.1 = (f32[64,128]{1,0:T(8,128)S(1)}, f32[64,128]{1,0:T(8,128)S(1)}, u32[]{:S(2)}, u32[]{:S(2)}) collective-permute-start(f32[64,128]{1,0:T(8,128)S(1)} %get-tuple-element.23.z_ref.z1_ref), channel_id=1, source_target_pairs={{8,16},{16,8},{9,17},{17,9},{10,18},{18,10},{11,19},{19,11},{12,20... | collective-permute-start | bytes 98312 | tf_op jit(solution)/shard_map/ppermute | solution.py:312
  36.2 0.9 collective-permute-start
  37.1 0.7 collective-permute-start.3
  37.8 0.0 collective-permute-done.2.s2
  37.8 1.6 %collective-permute-done.1.s1 = f32[64,128]{1,0:T(8,128)S(1)} collective-permute-done((f32[64,128]{1,0:T(8,128)S(1)}, f32[64,128]{1,0:T(8,128)S(1)}, u32[]{:S(2)}, u32[]{:S(2)}) %collective-permute-start.1) | collective-permute-done | bytes 32800 | tf_op jit(solution)/shard_map/ppermute | solution.py:312
  39.3 0.0 collective-permute-done.s0
  39.3 0.0 copy-done.1
  39.3 0.0 copy-done
  39.4 0.0 copy-done.2
  39.4 0.0 copy-done.3
  39.4 1.1 %own.2.own_ref = f32[64,128]{1,0:T(8,128)S(1)} custom-call(f32[64,128]{1,0:T(8,128)S(1)} %get-tuple-element.23.z_ref.z1_ref, bf16[64,64,128]{2,1,0:T(8,128)(2,1)S(1)} %copy-done.1, f32[64,128]{1,0:T(8,128)S(1)} %copy-done.2, f32[1,128]{1,0:T(1,128)S(1)} %bitcast.20, s32[4,128]{1,0:T(4,128)S(1)} %copy-done.3, f32[64,128]{1,0:T(8,128)S(1)} %collective-permute-done.s0, ...), custom_call_target="tpu_custom_call" | custom-call | tf_op jit(solution)/shard_map/own/pallas_call | solution.py:315
  40.4 0.0 collective-permute-done.3.s3
  40.4 0.8 image.1
  41.2 22.4 %all_to_all.34 = f32[256,1,128]{2,1,0:T(1,128)S(1)} all-to-all(f32[256,1,128]{2,1,0:T(1,128)S(1)} %bitcast.19), channel_id=1, replica_groups=mesh['gx'=32,'gy'=8] {'gx','gy'}, dimensions={0} | all-to-all | bytes 262144 | tf_op jit(solution)/shard_map/all_to_all | solution.py:286
  63.6 1.3 %second.1 = (f32[64,128]{1,0:T(8,128)S(1)}, f32[64,128]{1,0:T(8,128)S(1)}, f32[8,128]{1,0:T(8,128)S(1)}) custom-call(f32[64,128]{1,0:T(8,128)S(1)} %get-tuple-element.17.b_ref, f32[64,128]{1,0:T(8,128)S(1)} %get-tuple-element.24.w_ref, f32[8,128]{1,0:T(8,128)S(1)} %get-tuple-element.18.mask_ref, f32[128,128]{1,0:T(8,128)S(1)} %get-tuple-element.25.coarse_ref, ...), custom_call_target="tpu_custom_call" | custom-call | tf_op jit(solution)/shard_map/second/pallas_call | solution.py:325
  64.9 0.7 collective-permute-start.6
  65.6 2.1 %collective-permute-start.5 = (f32[64,128]{1,0:T(8,128)S(1)}, f32[64,128]{1,0:T(8,128)S(1)}, u32[]{:S(2)}, u32[]{:S(2)}) collective-permute-start(f32[64,128]{1,0:T(8,128)S(1)} %get-tuple-element.28.z_ref.z2_ref), channel_id=1, source_target_pairs={{8,16},{16,8},{9,17},{17,9},{10,18},{18,10},{11,19},{19,11},{12,20... | collective-permute-start | bytes 98312 | tf_op jit(solution)/shard_map/ppermute | solution.py:312
  67.6 0.9 collective-permute-start.4
  68.6 0.7 collective-permute-start.7
  69.2 0.0 collective-permute-done.6.s2
  69.2 1.6 %collective-permute-done.5.s1 = f32[64,128]{1,0:T(8,128)S(1)} collective-permute-done((f32[64,128]{1,0:T(8,128)S(1)}, f32[64,128]{1,0:T(8,128)S(1)}, u32[]{:S(2)}, u32[]{:S(2)}) %collective-permute-start.5) | collective-permute-done | bytes 32800 | tf_op jit(solution)/shard_map/ppermute | solution.py:312
  70.8 0.0 collective-permute-done.4.s0
  70.8 1.0 %own.3.own_ref = f32[64,128]{1,0:T(8,128)S(1)} custom-call(f32[64,128]{1,0:T(8,128)S(1)} %get-tuple-element.28.z_ref.z2_ref, bf16[64,64,128]{2,1,0:T(8,128)(2,1)S(1)} %copy-done.1, f32[64,128]{1,0:T(8,128)S(1)} %copy-done.2, f32[1,128]{1,0:T(1,128)S(1)} %bitcast.21, s32[4,128]{1,0:T(4,128)S(1)} %copy-done.3, f32[64,128]{1,0:T(8,128)S(1)} %collective-permute-done.4.s0, ...), custom_call_target="tpu_custom_call" | custom-call | tf_op jit(solution)/shard_map/own/pallas_call | solution.py:315
  71.9 0.0 collective-permute-done.7.s3
  71.9 0.5 last_image.1
  72.4 22.4 %all_to_all.35 = f32[256,1,128]{2,1,0:T(1,128)S(1)} all-to-all(f32[256,1,128]{2,1,0:T(1,128)S(1)} %bitcast.15), channel_id=1, replica_groups=mesh['gx'=32,'gy'=8] {'gx','gy'}, dimensions={0} | all-to-all | bytes 262144 | tf_op jit(solution)/shard_map/all_to_all | solution.py:286
  94.9 0.8 final.1
  (5 shorter events, 0.0 us)
Async XLA Ops:
  1.3 38.1 %copy-start.1 = (bf16[64,64,128]{2,1,0:T(8,128)(2,1)S(1)}, bf16[64,64,128]{2,1,0:T(8,128)(2,1)}, u32[]{:S(2)}) copy-start(bf16[64,64,128]{2,1,0:T(8,128)(2,1)} %blocks_ref.6) | copy-start | bytes 3145732
  32.2 7.2 %copy-start = (bf16[4,64,64,128]{3,2,1,0:T(8,128)(2,1)S(1)}, bf16[4,64,64,128]{3,2,1,0:T(8,128)(2,1)}, u32[]{:S(2)}) copy-start(bf16[4,64,64,128]{3,2,1,0:T(8,128)(2,1)} %blocks_ref.7) | copy-start | bytes 12582916
  32.2 7.2 %copy-start.2 = (f32[64,128]{1,0:T(8,128)S(1)}, f32[64,128]{1,0:T(8,128)}, u32[]{:S(2)}) copy-start(f32[64,128]{1,0:T(8,128)} %pressure_ref.3) | copy-start | bytes 98308
  32.2 7.2 %copy-start.3 = (s32[4,128]{1,0:T(4,128)S(1)}, s32[4,128]{1,0:T(4,128)}, u32[]{:S(2)}) copy-start(s32[4,128]{1,0:T(4,128)} %partners_ref.7) | copy-start | bytes 6148
  32.2 7.2 %copy-start.4 = (f32[128]{0:T(128)S(1)}, f32[128]{0:T(128)}, u32[]{:S(2)}) copy-start(f32[128]{0:T(128)} %param.12) | copy-start | bytes 1540
  33.4 4.3 %collective-permute-start.2 = (f32[64,128]{1,0:T(8,128)S(1)}, f32[64,128]{1,0:T(8,128)S(1)}, u32[]{:S(2)}, u32[]{:S(2)}) collective-permute-start(f32[64,128]{1,0:T(8,128)S(1)} %get-tuple-element.23.z_ref.z1_ref), channel_id=1, source_target_pairs={{0,8},{8,0},{1,9},{9,1},{2,10},{10,2},{3,11},{11,3},{4,12},{12,4},... | collective-permute-start | bytes 98312 | tf_op jit(solution)/shard_map/ppermute | solution.py:312
  34.1 5.2 %collective-permute-start.1 = (f32[64,128]{1,0:T(8,128)S(1)}, f32[64,128]{1,0:T(8,128)S(1)}, u32[]{:S(2)}, u32[]{:S(2)}) collective-permute-start(f32[64,128]{1,0:T(8,128)S(1)} %get-tuple-element.23.z_ref.z1_ref), channel_id=1, source_target_pairs={{8,16},{16,8},{9,17},{17,9},{10,18},{18,10},{11,19},{19,11},{12,20... | collective-permute-start | bytes 98312 | tf_op jit(solution)/shard_map/ppermute | solution.py:312
  36.2 3.2 %collective-permute-start = (f32[64,128]{1,0:T(8,128)S(1)}, f32[64,128]{1,0:T(8,128)S(1)}, u32[]{:S(2)}, u32[]{:S(2)}) collective-permute-start(f32[64,128]{1,0:T(8,128)S(1)} %get-tuple-element.23.z_ref.z1_ref), channel_id=1, source_target_pairs={{0,1},{1,0},{2,3},{3,2},{4,5},{5,4},{6,7},{7,6},{8,9},{9,8},{10,11... | collective-permute-start | bytes 98312 | tf_op jit(solution)/shard_map/ppermute | solution.py:312
  37.1 3.3 %collective-permute-start.3 = (f32[64,128]{1,0:T(8,128)S(1)}, f32[64,128]{1,0:T(8,128)S(1)}, u32[]{:S(2)}, u32[]{:S(2)}) collective-permute-start(f32[64,128]{1,0:T(8,128)S(1)} %get-tuple-element.23.z_ref.z1_ref), channel_id=1, source_target_pairs={{1,2},{2,1},{3,4},{4,3},{5,6},{6,5},{9,10},{10,9},{11,12},{12,11},... | collective-permute-start | bytes 98312 | tf_op jit(solution)/shard_map/ppermute | solution.py:312
  64.9 4.3 %collective-permute-start.6 = (f32[64,128]{1,0:T(8,128)S(1)}, f32[64,128]{1,0:T(8,128)S(1)}, u32[]{:S(2)}, u32[]{:S(2)}) collective-permute-start(f32[64,128]{1,0:T(8,128)S(1)} %get-tuple-element.28.z_ref.z2_ref), channel_id=1, source_target_pairs={{0,8},{8,0},{1,9},{9,1},{2,10},{10,2},{3,11},{11,3},{4,12},{12,4},... | collective-permute-start | bytes 98312 | tf_op jit(solution)/shard_map/ppermute | solution.py:312
  65.6 5.2 %collective-permute-start.5 = (f32[64,128]{1,0:T(8,128)S(1)}, f32[64,128]{1,0:T(8,128)S(1)}, u32[]{:S(2)}, u32[]{:S(2)}) collective-permute-start(f32[64,128]{1,0:T(8,128)S(1)} %get-tuple-element.28.z_ref.z2_ref), channel_id=1, source_target_pairs={{8,16},{16,8},{9,17},{17,9},{10,18},{18,10},{11,19},{19,11},{12,20... | collective-permute-start | bytes 98312 | tf_op jit(solution)/shard_map/ppermute | solution.py:312
  67.6 3.2 %collective-permute-start.4 = (f32[64,128]{1,0:T(8,128)S(1)}, f32[64,128]{1,0:T(8,128)S(1)}, u32[]{:S(2)}, u32[]{:S(2)}) collective-permute-start(f32[64,128]{1,0:T(8,128)S(1)} %get-tuple-element.28.z_ref.z2_ref), channel_id=1, source_target_pairs={{0,1},{1,0},{2,3},{3,2},{4,5},{5,4},{6,7},{7,6},{8,9},{9,8},{10,11... | collective-permute-start | bytes 98312 | tf_op jit(solution)/shard_map/ppermute | solution.py:312
  68.6 3.3 %collective-permute-start.7 = (f32[64,128]{1,0:T(8,128)S(1)}, f32[64,128]{1,0:T(8,128)S(1)}, u32[]{:S(2)}, u32[]{:S(2)}) collective-permute-start(f32[64,128]{1,0:T(8,128)S(1)} %get-tuple-element.28.z_ref.z2_ref), channel_id=1, source_target_pairs={{1,2},{2,1},{3,4},{4,3},{5,6},{6,5},{9,10},{10,9},{11,12},{12,11},... | collective-permute-start | bytes 98312 | tf_op jit(solution)/shard_map/ppermute | solution.py:312

commit v4 on v3

--- a/solution.py
+++ b/solution.py
@@ -72,10 +72,15 @@
             partial_ref[rows, :] = jnp.zeros((8, SLOTS), F32)
 
 
+def apply_local(local_ref, v_ref, partial_ref):
+    blocks_into(partial_ref, [(lambda i: local_ref[i], lambda: v_ref[...])])
+    return fold_rows(partial_ref, NODES)
+
+
 def restrict_kernel(
     count_ref, rhs_hbm, basis_hbm, local_hbm, inverse_hbm,
-    row_ref, b_ref, mask_ref, basis_ref, local_ref, inverse_ref,
-    partial_ref, rhs_sem, basis_sem, local_sem, inverse_sem,
+    row_ref, b_ref, mask_ref, local_b_ref, basis_ref, local_ref, inverse_ref,
+    partial_ref, other_ref, rhs_sem, basis_sem, local_sem, inverse_sem,
 ):
     rhs_copy = pltpu.make_async_copy(rhs_hbm, b_ref, rhs_sem)
     rhs_copy.start()
@@ -100,6 +105,7 @@
         )
     send_row(partial_ref, row_ref)
     local_copy.wait()
+    local_b_ref[...] = apply_local(local_ref, b_ref, other_ref)
     inverse_copy.wait()
 
 
@@ -110,28 +116,25 @@
     return jnp.where(lane < MODES, even, pltpu.roll(odd, MODES, 1))
 
 
-def precondition(v_ref, coarse_ref, inverse_ref, local_ref, basis_ref, partial_ref, modal_ref):
+def coarse_part(start, coarse_ref, inverse_ref, basis_ref, modal_ref):
     def coarse_step(t, acc):
         column = inverse_ref[:, pl.ds(pl.multiple_of(t * SLOTS, SLOTS), SLOTS)].astype(F32)
         return acc + column * coarse_ref[pl.ds(t, 1), :]
 
     acc = lax.fori_loop(0, 2 * MODES, coarse_step, jnp.zeros((MODES, SLOTS), F32), unroll=2 * UNROLL)
     modal_ref[...] = jnp.broadcast_to(jnp.sum(acc, axis=1, keepdims=True), (MODES, SLOTS))
-    blocks_into(partial_ref, [(lambda i: local_ref[i], lambda: v_ref[...])])
 
     def prolong_step(m, total):
         return total + basis_ref[m].astype(F32) * modal_ref[pl.ds(m, 1), :]
 
-    total = lax.fori_loop(0, MODES, prolong_step, jnp.zeros((NODES, SLOTS), F32), unroll=2 * UNROLL)
-    return total + fold_rows(partial_ref, NODES)
+    return lax.fori_loop(0, MODES, prolong_step, start, unroll=2 * UNROLL)
 
 
 def first_kernel(
-    mask_ref, b_ref, gathered_ref, inverse_ref, local_ref, basis_ref,
-    z_ref, coarse_ref, partial_ref, modal_ref,
+    mask_ref, local_b_ref, gathered_ref, inverse_ref, basis_ref, z_ref, coarse_ref, modal_ref
 ):
     coarse_ref[...] = halves(gathered_ref)
-    z = precondition(b_ref, coarse_ref, inverse_ref, local_ref, basis_ref, partial_ref, modal_ref)
+    z = coarse_part(local_b_ref[...], coarse_ref, inverse_ref, basis_ref, modal_ref)
     z_ref[...] = z * mask_ref[0:1, :]
 
 
@@ -141,17 +144,18 @@
 
 
 def second_kernel(
-    b_ref, w_ref, mask_ref, coarse_ref, gathered_ref, inverse_ref, local_ref, basis_ref,
-    z_ref, v_ref, sums_ref, mixed_ref, partial_ref, modal_ref,
+    b_ref, w_ref, mask_ref, z1_ref, gathered_ref, inverse_ref, local_ref, basis_ref,
+    z_ref, v_ref, sums_ref, coarse_ref, partial_ref, modal_ref,
 ):
     sums = jnp.sum(gathered_ref[...], axis=0, keepdims=True)
     sums_ref[...] = jnp.broadcast_to(sums, sums_ref.shape)
     along = lane_of(sums, MODES) / lane_of(sums, MODES + 2)
     scale = 1.0 / jnp.sqrt(lane_of(sums, MODES + 1))
-    mixed_ref[...] = (halves(gathered_ref) - along * coarse_ref[...]) * scale
     v_ref[...] = (w_ref[...] - along * b_ref[...]) * scale
-    z = precondition(v_ref, mixed_ref, inverse_ref, local_ref, basis_ref, partial_ref, modal_ref)
-    z_ref[...] = z * mask_ref[0:1, :]
+    coarse_ref[...] = halves(gathered_ref)
+    local_part = apply_local(local_ref, w_ref, partial_ref)
+    z = coarse_part(local_part, coarse_ref, inverse_ref, basis_ref, modal_ref)
+    z_ref[...] = (z * mask_ref[0:1, :] - along * z1_ref[...]) * scale
 
 
 def face_of(q):
@@ -176,10 +180,9 @@
     return terms
 
 
-def own_kernel(
-    z_ref, blocks_ref, pressure_ref, alpha_ref, partners_ref, s0, s1, s2, faces_ref, out_ref, picked_ref, partial_ref
-):
-    terms = face_terms(EARLY, (s0, s1, s2), partners_ref, faces_ref, picked_ref)
+def own_kernel(z_ref, blocks_ref, pressure_ref, alpha_ref, partners_ref, *refs):
+    source_refs, (faces_ref, out_ref, picked_ref, partial_ref) = refs[: len(EARLY)], refs[len(EARLY) :]
+    terms = face_terms(EARLY, source_refs, partners_ref, faces_ref, picked_ref)
     blocks_into(partial_ref, [(lambda i: blocks_ref[i], lambda: z_ref[...])] + terms)
     alpha = alpha_ref[...]
     scaled = jnp.abs(alpha * pressure_ref[...])
@@ -189,16 +192,15 @@
     out_ref[...] = fold_rows(partial_ref, NODES) + storage * z_ref[...]
 
 
-def all_blocks(own_ref, mask_ref, partners_ref, source_ref, faces_ref, picked_ref, partial_ref):
-    blocks_into(partial_ref, face_terms(LATER, (source_ref,), partners_ref, faces_ref, picked_ref))
+def all_blocks(own_ref, mask_ref, partners_ref, source_refs, faces_ref, picked_ref, partial_ref):
+    blocks_into(partial_ref, face_terms(LATER, source_refs, partners_ref, faces_ref, picked_ref))
     return (own_ref[...] + fold_rows(partial_ref, NODES)) * mask_ref[0:1, :]
 
 
-def image_kernel(
-    own_ref, mask_ref, partners_ref, s3, blocks_ref, b_ref, basis_ref,
-    w_ref, row_ref, picked_ref, partial_ref,
-):
-    w_ref[...] = all_blocks(own_ref, mask_ref, partners_ref, s3, blocks_ref, picked_ref, partial_ref)
+def image_kernel(own_ref, mask_ref, partners_ref, *refs):
+    source_refs, refs = refs[: len(LATER)], refs[len(LATER) :]
+    blocks_ref, b_ref, basis_ref, w_ref, row_ref, picked_ref, partial_ref = refs
+    w_ref[...] = all_blocks(own_ref, mask_ref, partners_ref, source_refs, blocks_ref, picked_ref, partial_ref)
     blocks_into(partial_ref, [(lambda m: basis_ref[m], lambda: w_ref[...])])
     w = w_ref[...]
     b = b_ref[...]
@@ -206,11 +208,10 @@
     send_row(partial_ref, row_ref)
 
 
-def last_image_kernel(
-    own_ref, mask_ref, partners_ref, s3, blocks_ref, b_ref, v_ref,
-    row_ref, picked_ref, partial_ref,
-):
-    w = all_blocks(own_ref, mask_ref, partners_ref, s3, blocks_ref, picked_ref, partial_ref)
+def last_image_kernel(own_ref, mask_ref, partners_ref, *refs):
+    source_refs, refs = refs[: len(LATER)], refs[len(LATER) :]
+    blocks_ref, b_ref, v_ref, row_ref, picked_ref, partial_ref = refs
+    w = all_blocks(own_ref, mask_ref, partners_ref, source_refs, blocks_ref, picked_ref, partial_ref)
     b = b_ref[...]
     v = v_ref[...]
     partial_ref[pl.ds(0, 8 * MODES), :] = jnp.zeros((8 * MODES, SLOTS), F32)
@@ -297,41 +298,40 @@
         in_hbm = lambda x: pltpu.with_memory_space_constraint(x, pltpu.HBM)
         held = lambda x: jax.ShapeDtypeStruct(x.shape, x.dtype)
         semaphore = pltpu.SemaphoreType.DMA
-        rows, b, mask, basis, local, inverse = call(
+        rows, b, mask, local_b, basis, local, inverse = call(
             restrict_kernel, "restrict", [pl.BlockSpec(memory_space=pltpu.SMEM)] + [HB] * 4,
-            (vec(total, SLOTS), held(right_side), vec(8, SLOTS), held(coarse_basis), held(local_inverse), held(coarse_inverse)),
-            [partial, semaphore, semaphore((PIECES,)), semaphore, semaphore],
+            (vec(total, SLOTS), held(right_side), vec(8, SLOTS), vec(NODES, SLOTS), held(coarse_basis), held(local_inverse), held(coarse_inverse)),
+            [partial, partial, semaphore, semaphore((PIECES,)), semaphore, semaphore],
         )(live_counts, *(in_hbm(x) for x in (right_side, coarse_basis, local_inverse, coarse_inverse)))
         gathered = exchange(rows)
-        z1, coarse = call(
-            first_kernel, "first", [VM] * 6,
-            (vec(NODES, SLOTS), vec(SLOTS, SLOTS)), [partial, modal],
-        )(mask, b, gathered, inverse, local, basis)
+        z1 = call(
+            first_kernel, "first", [VM] * 5, vec(NODES, SLOTS), [pltpu.VMEM((SLOTS, SLOTS), F32), modal]
+        )(mask, local_b, gathered, inverse, basis)
 
         def neighbours(z):
             return [lax.ppermute(z, axes, pairs[q]) for q in EARLY + LATER]
 
         def own(z, sources):
-            return call(own_kernel, "own", [VM] * 9, vec(NODES, SLOTS), [picked, partial])(
+            return call(own_kernel, "own", [VM] * (6 + len(EARLY)), vec(NODES, SLOTS), [picked, partial])(
                 z, element_blocks, pressure_head, alpha, partners, *sources, face_blocks
             )
 
         sources = neighbours(z1)
         w1, rows = call(
-            image_kernel, "image", [VM] * 7,
+            image_kernel, "image", [VM] * (6 + len(LATER)),
             (vec(NODES, SLOTS), vec(total, SLOTS)), [picked, partial],
-        )(own(z1, sources[:3]), mask, partners, sources[3], face_blocks, b, basis)
+        )(own(z1, sources[: len(EARLY)]), mask, partners, *sources[len(EARLY) :], face_blocks, b, basis)
         gathered = exchange(rows)
         z2, v2, sums = call(
             second_kernel, "second", [VM] * 8,
             (vec(NODES, SLOTS), vec(NODES, SLOTS), vec(8, SLOTS)),
             [pltpu.VMEM((SLOTS, SLOTS), F32), partial, modal],
-        )(b, w1, mask, coarse, gathered, inverse, local, basis)
+        )(b, w1, mask, z1, gathered, inverse, local, basis)
         sources = neighbours(z2)
         rows = call(
-            last_image_kernel, "last_image", [VM] * 7,
+            last_image_kernel, "last_image", [VM] * (6 + len(LATER)),
             vec(total, SLOTS), [picked, partial],
-        )(own(z2, sources[:3]), mask, partners, sources[3], face_blocks, b, v2)
+        )(own(z2, sources[: len(EARLY)]), mask, partners, *sources[len(EARLY) :], face_blocks, b, v2)
         gathered = exchange(rows)
         update, hess = call(
             final_kernel, "final", [VM] * 4, (vec(NODES, SLOTS), vec(2, 3)), []

time: 95.9 us -> 95.7 us (level)
  no operation moved by 1% of the time
where the time goes in v4:
time: 95.7 us; the launch traced here: 95.5 us
  blocking collectives  73.3 us (77%)
  Pallas kernels  8.88 us (9%)
  starting transfers between devices  8.63 us (9%)
  waiting for transfers between devices  3.13 us (3%)
  between operations  1.46 us (2%)
    all_to_all x3, blocking collectives, exchange(): return lax.all_to_all(rows, axes, 0, 0, tiled=True)  73.3 us
    ppermute x8, starting transfers between devices, neighbours(): return [lax.ppermute(z, axes, pairs[q]) for q in EARLY + LATER]  8.63 us
    ppermute x8, waiting for transfers between devices, neighbours(): return [lax.ppermute(z, axes, pairs[q]) for q in EARLY + LATER]  3.13 us
    pallas_call x1, Pallas kernels, shards(): call(restrict_kernel, 'restrict', [pl.BlockSpec(memory_space=pltpu.SMEM)]...  2.45 us
    pallas_call x2, Pallas kernels, own(): call(own_kernel, 'own', [VM] * (6 + len(EARLY)), vec(NODES, SLOTS), [pick...  2.09 us
  transfers between devices with their start and end apart: 8, of which 2 were waited for; matrix products, arithmetic and copies ran while one was open for 0% of the time, Pallas kernels for 2%

profile of v4, /device:TPU:1, one launch (start us, length us, event | category | flops | bytes accessed | tf_op | source)
XLA Modules:
  0.0 95.5 jit_solution(8242518397988994583)
XLA Ops:
  1.3 0.0 copy-start
  1.3 2.5 %restrict.1 = (f32[256,128]{1,0:T(8,128)S(1)}, f32[64,128]{1,0:T(8,128)S(1)}, f32[8,128]{1,0:T(8,128)S(1)}, f32[64,128]{1,0:T(8,128)S(1)}, bf16[64,64,128]{2,1,0...) custom-call(s32[1]{0:T(128)S(6)} %copy.15.count_ref, f32[64,128]{1,0:T(8,128)} %rhs_hbm.1, ...), custom_call_target="tpu_custom_call" | custom-call | tf_op jit(solution)/shard_map/restrict/pallas_call | solution.py:301
  3.7 0.0 copy-start.1
  3.8 0.0 copy-start.2
  3.8 0.0 copy-start.3
  3.8 0.0 copy-start.4
  3.8 28.5 %all_to_all.33 = f32[256,1,128]{2,1,0:T(1,128)S(1)} all-to-all(f32[256,1,128]{2,1,0:T(1,128)S(1)} %bitcast.18), channel_id=1, replica_groups=mesh['gx'=32,'gy'=8] {'gx','gy'}, dimensions={0} | all-to-all | bytes 262144 | tf_op jit(solution)/shard_map/all_to_all | solution.py:287
  32.3 1.0 %first.1.z_ref.z1_ref = f32[64,128]{1,0:T(8,128)S(1)} custom-call(f32[8,128]{1,0:T(8,128)S(1)} %get-tuple-element.17.mask_ref, f32[64,128]{1,0:T(8,128)S(1)} %get-tuple-element.18.local_b_ref, f32[256,128]{1,0:T(8,128)S(1)} %bitcast.16, bf16[64,16384]{1,0:T(8,128)(2,1)S(1)} %get-tuple-element.20.inverse_ref, ...), custom_call_target="tpu_custom_call" | custom-call | tf_op jit(solution)/shard_map/first/pallas_call | solution.py:307
  33.3 0.7 collective-permute-start.2
  33.9 2.1 %collective-permute-start.1 = (f32[64,128]{1,0:T(8,128)S(1)}, f32[64,128]{1,0:T(8,128)S(1)}, u32[]{:S(2)}, u32[]{:S(2)}) collective-permute-start(f32[64,128]{1,0:T(8,128)S(1)} %first.1.z_ref.z1_ref), channel_id=1, source_target_pairs={{8,16},{16,8},{9,17},{17,9},{10,18},{18,10},{11,19},{19,11},{12,20... | collective-permute-start | bytes 98312 | tf_op jit(solution)/shard_map/ppermute | solution.py:312
  36.0 0.9 collective-permute-start
  36.9 0.7 collective-permute-start.3
  37.6 0.0 collective-permute-done.2.refs_2_
  37.6 1.6 %collective-permute-done.1.refs_1_ = f32[64,128]{1,0:T(8,128)S(1)} collective-permute-done((f32[64,128]{1,0:T(8,128)S(1)}, f32[64,128]{1,0:T(8,128)S(1)}, u32[]{:S(2)}, u32[]{:S(2)}) %collective-permute-start.1) | collective-permute-done | bytes 32800 | tf_op jit(solution)/shard_map/ppermute | solution.py:312
  39.2 0.0 collective-permute-done.refs_0_
  39.2 1.1 %own.2.own_ref = f32[64,128]{1,0:T(8,128)S(1)} custom-call(f32[64,128]{1,0:T(8,128)S(1)} %first.1.z_ref.z1_ref, bf16[64,64,128]{2,1,0:T(8,128)(2,1)S(1)} %copy-done.1, f32[64,128]{1,0:T(8,128)S(1)} %copy-done.2, f32[1,128]{1,0:T(1,128)S(1)} %bitcast.20, s32[4,128]{1,0:T(4,128)S(1)} %copy-done.3, f32[64,128]{1,0:T(8,128)S(1)} %collective-permute-done.refs_0_, ...), custom_call_target="tpu_custom_call" | custom-call | tf_op jit(solution)/shard_map/own/pallas_call | solution.py:315
  40.3 0.0 collective-permute-done.3.refs_0_
  40.3 0.8 image.1
  41.0 22.4 %all_to_all.34 = f32[256,1,128]{2,1,0:T(1,128)S(1)} all-to-all(f32[256,1,128]{2,1,0:T(1,128)S(1)} %bitcast.19), channel_id=1, replica_groups=mesh['gx'=32,'gy'=8] {'gx','gy'}, dimensions={0} | all-to-all | bytes 262144 | tf_op jit(solution)/shard_map/all_to_all | solution.py:287
  63.4 1.3 %second.1 = (f32[64,128]{1,0:T(8,128)S(1)}, f32[64,128]{1,0:T(8,128)S(1)}, f32[8,128]{1,0:T(8,128)S(1)}) custom-call(f32[64,128]{1,0:T(8,128)S(1)} %get-tuple-element.16.refs_2_.b_ref, f32[64,128]{1,0:T(8,128)S(1)} %get-tuple-element.22.w_ref, f32[8,128]{1,0:T(8,128)S(1)} %get-tuple-element.17.mask_ref, f32[64,128]{1,0:T(8,128)S(1)} %first.1.z_ref.z1_ref, ...), custom_call_target="tpu_custom_call" | custom-call | tf_op jit(solution)/shard_map/second/pallas_call | solution.py:325
  64.7 0.7 collective-permute-start.6
  65.4 2.1 %collective-permute-start.5 = (f32[64,128]{1,0:T(8,128)S(1)}, f32[64,128]{1,0:T(8,128)S(1)}, u32[]{:S(2)}, u32[]{:S(2)}) collective-permute-start(f32[64,128]{1,0:T(8,128)S(1)} %get-tuple-element.26.z_ref.z2_ref), channel_id=1, source_target_pairs={{8,16},{16,8},{9,17},{17,9},{10,18},{18,10},{11,19},{19,11},{12,20... | collective-permute-start | bytes 98312 | tf_op jit(solution)/shard_map/ppermute | solution.py:312
  67.5 0.9 collective-permute-start.4
  68.4 0.7 collective-permute-start.7
  69.1 0.0 collective-permute-done.6.refs_2_
  69.1 1.6 %collective-permute-done.5.refs_1_ = f32[64,128]{1,0:T(8,128)S(1)} collective-permute-done((f32[64,128]{1,0:T(8,128)S(1)}, f32[64,128]{1,0:T(8,128)S(1)}, u32[]{:S(2)}, u32[]{:S(2)}) %collective-permute-start.5) | collective-permute-done | bytes 32800 | tf_op jit(solution)/shard_map/ppermute | solution.py:312
  70.6 0.0 collective-permute-done.4.refs_0_
  70.6 1.0 %own.3.own_ref = f32[64,128]{1,0:T(8,128)S(1)} custom-call(f32[64,128]{1,0:T(8,128)S(1)} %get-tuple-element.26.z_ref.z2_ref, bf16[64,64,128]{2,1,0:T(8,128)(2,1)S(1)} %copy-done.1, f32[64,128]{1,0:T(8,128)S(1)} %copy-done.2, f32[1,128]{1,0:T(1,128)S(1)} %bitcast.21, s32[4,128]{1,0:T(4,128)S(1)} %copy-done.3, f32[64,128]{1,0:T(8,128)S(1)} %collective-permute-done.4.refs_0_, ...), custom_call_target="tpu_custom_call" | custom-call | tf_op jit(solution)/shard_map/own/pallas_call | solution.py:315
  71.7 0.0 collective-permute-done.7.refs_0_
  71.7 0.5 last_image.1
  72.2 22.4 %all_to_all.35 = f32[256,1,128]{2,1,0:T(1,128)S(1)} all-to-all(f32[256,1,128]{2,1,0:T(1,128)S(1)} %bitcast.15), channel_id=1, replica_groups=mesh['gx'=32,'gy'=8] {'gx','gy'}, dimensions={0} | all-to-all | bytes 262144 | tf_op jit(solution)/shard_map/all_to_all | solution.py:287
  94.7 0.8 final.1
  (5 shorter events, 0.0 us)
Async XLA Ops:
  1.3 37.9 %copy-start = (bf16[4,64,64,128]{3,2,1,0:T(8,128)(2,1)S(1)}, bf16[4,64,64,128]{3,2,1,0:T(8,128)(2,1)}, u32[]{:S(2)}) copy-start(bf16[4,64,64,128]{3,2,1,0:T(8,128)(2,1)} %refs_1_.3) | copy-start | bytes 12582916
  3.7 35.4 %copy-start.1 = (bf16[64,64,128]{2,1,0:T(8,128)(2,1)S(1)}, bf16[64,64,128]{2,1,0:T(8,128)(2,1)}, u32[]{:S(2)}) copy-start(bf16[64,64,128]{2,1,0:T(8,128)(2,1)} %blocks_ref.3) | copy-start | bytes 3145732
  3.8 35.4 %copy-start.2 = (f32[64,128]{1,0:T(8,128)S(1)}, f32[64,128]{1,0:T(8,128)}, u32[]{:S(2)}) copy-start(f32[64,128]{1,0:T(8,128)} %pressure_ref.3) | copy-start | bytes 98308
  3.8 35.4 %copy-start.3 = (s32[4,128]{1,0:T(4,128)S(1)}, s32[4,128]{1,0:T(4,128)}, u32[]{:S(2)}) copy-start(s32[4,128]{1,0:T(4,128)} %partners_ref.7) | copy-start | bytes 6148
  3.8 35.4 %copy-start.4 = (f32[128]{0:T(128)S(1)}, f32[128]{0:T(128)}, u32[]{:S(2)}) copy-start(f32[128]{0:T(128)} %param.12) | copy-start | bytes 1540
  33.3 4.3 %collective-permute-start.2 = (f32[64,128]{1,0:T(8,128)S(1)}, f32[64,128]{1,0:T(8,128)S(1)}, u32[]{:S(2)}, u32[]{:S(2)}) collective-permute-start(f32[64,128]{1,0:T(8,128)S(1)} %first.1.z_ref.z1_ref), channel_id=1, source_target_pairs={{0,8},{8,0},{1,9},{9,1},{2,10},{10,2},{3,11},{11,3},{4,12},{12,4},... | collective-permute-start | bytes 98312 | tf_op jit(solution)/shard_map/ppermute | solution.py:312
  33.9 5.2 %collective-permute-start.1 = (f32[64,128]{1,0:T(8,128)S(1)}, f32[64,128]{1,0:T(8,128)S(1)}, u32[]{:S(2)}, u32[]{:S(2)}) collective-permute-start(f32[64,128]{1,0:T(8,128)S(1)} %first.1.z_ref.z1_ref), channel_id=1, source_target_pairs={{8,16},{16,8},{9,17},{17,9},{10,18},{18,10},{11,19},{19,11},{12,20... | collective-permute-start | bytes 98312 | tf_op jit(solution)/shard_map/ppermute | solution.py:312
  36.0 3.2 %collective-permute-start = (f32[64,128]{1,0:T(8,128)S(1)}, f32[64,128]{1,0:T(8,128)S(1)}, u32[]{:S(2)}, u32[]{:S(2)}) collective-permute-start(f32[64,128]{1,0:T(8,128)S(1)} %first.1.z_ref.z1_ref), channel_id=1, source_target_pairs={{0,1},{1,0},{2,3},{3,2},{4,5},{5,4},{6,7},{7,6},{8,9},{9,8},{10,11... | collective-permute-start | bytes 98312 | tf_op jit(solution)/shard_map/ppermute | solution.py:312
  36.9 3.3 %collective-permute-start.3 = (f32[64,128]{1,0:T(8,128)S(1)}, f32[64,128]{1,0:T(8,128)S(1)}, u32[]{:S(2)}, u32[]{:S(2)}) collective-permute-start(f32[64,128]{1,0:T(8,128)S(1)} %first.1.z_ref.z1_ref), channel_id=1, source_target_pairs={{1,2},{2,1},{3,4},{4,3},{5,6},{6,5},{9,10},{10,9},{11,12},{12,11},... | collective-permute-start | bytes 98312 | tf_op jit(solution)/shard_map/ppermute | solution.py:312
  64.7 4.3 %collective-permute-start.6 = (f32[64,128]{1,0:T(8,128)S(1)}, f32[64,128]{1,0:T(8,128)S(1)}, u32[]{:S(2)}, u32[]{:S(2)}) collective-permute-start(f32[64,128]{1,0:T(8,128)S(1)} %get-tuple-element.26.z_ref.z2_ref), channel_id=1, source_target_pairs={{0,8},{8,0},{1,9},{9,1},{2,10},{10,2},{3,11},{11,3},{4,12},{12,4},... | collective-permute-start | bytes 98312 | tf_op jit(solution)/shard_map/ppermute | solution.py:312
  65.4 5.2 %collective-permute-start.5 = (f32[64,128]{1,0:T(8,128)S(1)}, f32[64,128]{1,0:T(8,128)S(1)}, u32[]{:S(2)}, u32[]{:S(2)}) collective-permute-start(f32[64,128]{1,0:T(8,128)S(1)} %get-tuple-element.26.z_ref.z2_ref), channel_id=1, source_target_pairs={{8,16},{16,8},{9,17},{17,9},{10,18},{18,10},{11,19},{19,11},{12,20... | collective-permute-start | bytes 98312 | tf_op jit(solution)/shard_map/ppermute | solution.py:312
  67.5 3.2 %collective-permute-start.4 = (f32[64,128]{1,0:T(8,128)S(1)}, f32[64,128]{1,0:T(8,128)S(1)}, u32[]{:S(2)}, u32[]{:S(2)}) collective-permute-start(f32[64,128]{1,0:T(8,128)S(1)} %get-tuple-element.26.z_ref.z2_ref), channel_id=1, source_target_pairs={{0,1},{1,0},{2,3},{3,2},{4,5},{5,4},{6,7},{7,6},{8,9},{9,8},{10,11... | collective-permute-start | bytes 98312 | tf_op jit(solution)/shard_map/ppermute | solution.py:312
  68.4 3.3 %collective-permute-start.7 = (f32[64,128]{1,0:T(8,128)S(1)}, f32[64,128]{1,0:T(8,128)S(1)}, u32[]{:S(2)}, u32[]{:S(2)}) collective-permute-start(f32[64,128]{1,0:T(8,128)S(1)} %get-tuple-element.26.z_ref.z2_ref), channel_id=1, source_target_pairs={{1,2},{2,1},{3,4},{4,3},{5,6},{6,5},{9,10},{10,9},{11,12},{12,11},... | collective-permute-start | bytes 98312 | tf_op jit(solution)/shard_map/ppermute | solution.py:312

commit v5 on v4

--- a/solution.py
+++ b/solution.py
@@ -18,7 +18,7 @@
 VM = pl.BlockSpec(memory_space=pltpu.VMEM)
 HB = pl.BlockSpec(memory_space=pltpu.HBM)
 PIECES = 4
-UNROLL = 8
+UNROLL = 16
 EARLY = (2, 1, 0)
 LATER = (3,)
 
@@ -75,6 +75,15 @@
 def apply_local(local_ref, v_ref, partial_ref):
     blocks_into(partial_ref, [(lambda i: local_ref[i], lambda: v_ref[...])])
     return fold_rows(partial_ref, NODES)
+
+
+def send_dots(pairs, out_ref):
+    lane = lax.broadcasted_iota(jnp.int32, (1, SLOTS), 1)
+    row = jnp.zeros((1, SLOTS), F32)
+    for k, (left, right) in enumerate(pairs):
+        total = jnp.sum(jnp.sum(tile_sum(left * right), axis=0, keepdims=True), axis=1, keepdims=True)
+        row = jnp.where(lane == MODES + k, total, row)
+    out_ref[...] = jnp.broadcast_to(row, out_ref.shape)
 
 
 def restrict_kernel(
@@ -214,9 +223,7 @@
     w = all_blocks(own_ref, mask_ref, partners_ref, source_refs, blocks_ref, picked_ref, partial_ref)
     b = b_ref[...]
     v = v_ref[...]
-    partial_ref[pl.ds(0, 8 * MODES), :] = jnp.zeros((8 * MODES, SLOTS), F32)
-    put_dots(partial_ref, [(w, b), (w, v), (w, w), (v, v), (b, v)])
-    send_row(partial_ref, row_ref)
+    send_dots([(w, b), (w, v), (w, w), (v, v), (b, v)], row_ref)
 
 
 def final_kernel(first_ref, gathered_ref, z1_ref, z2_ref, update_ref, hess_ref):

time: 95.7 us -> 95.5 us (level)
  no operation moved by 1% of the time
where the time goes in v5:
time: 95.5 us; the launch traced here: 95.2 us
  blocking collectives  73.4 us (77%)
  starting transfers between devices  8.63 us (9%)
  Pallas kernels  8.6 us (9%)
  waiting for transfers between devices  3.13 us (3%)
  between operations  1.45 us (2%)
    all_to_all x3, blocking collectives, exchange(): return lax.all_to_all(rows, axes, 0, 0, tiled=True)  73.4 us
    ppermute x8, starting transfers between devices, neighbours(): return [lax.ppermute(z, axes, pairs[q]) for q in EARLY + LATER]  8.63 us
    ppermute x8, waiting for transfers between devices, neighbours(): return [lax.ppermute(z, axes, pairs[q]) for q in EARLY + LATER]  3.13 us
    pallas_call x1, Pallas kernels, shards(): call(restrict_kernel, 'restrict', [pl.BlockSpec(memory_space=pltpu.SMEM)]...  2.45 us
    pallas_call x2, Pallas kernels, own(): call(own_kernel, 'own', [VM] * (6 + len(EARLY)), vec(NODES, SLOTS), [pick...  2.03 us
  transfers between devices with their start and end apart: 8, of which 2 were waited for; matrix products, arithmetic and copies ran while one was open for 0% of the time, Pallas kernels for 2%

profile of v5, /device:TPU:1, one launch (start us, length us, event | category | flops | bytes accessed | tf_op | source)
XLA Modules:
  0.0 95.2 jit_solution(18214556485438102496)
XLA Ops:
  1.3 2.5 %restrict.1 = (f32[256,128]{1,0:T(8,128)S(1)}, f32[64,128]{1,0:T(8,128)S(1)}, f32[8,128]{1,0:T(8,128)S(1)}, f32[64,128]{1,0:T(8,128)S(1)}, bf16[64,64,128]{2,1,0...) custom-call(s32[1]{0:T(128)S(6)} %copy.15.count_ref, f32[64,128]{1,0:T(8,128)} %rhs_hbm.1, ...), custom_call_target="tpu_custom_call" | custom-call | tf_op jit(solution)/shard_map/restrict/pallas_call | solution.py:308
  3.7 0.0 copy-start.1
  3.8 0.0 copy-start.2
  3.8 0.0 copy-start.3
  3.8 0.0 copy-start.4
  3.8 28.5 %all_to_all.33 = f32[256,1,128]{2,1,0:T(1,128)S(1)} all-to-all(f32[256,1,128]{2,1,0:T(1,128)S(1)} %bitcast.18), channel_id=1, replica_groups=mesh['gx'=32,'gy'=8] {'gx','gy'}, dimensions={0} | all-to-all | bytes 262144 | tf_op jit(solution)/shard_map/all_to_all | solution.py:294
  32.3 0.9 first.1.z_ref.z1_ref
  33.2 0.7 collective-permute-start.2
  33.9 2.1 %collective-permute-start.1 = (f32[64,128]{1,0:T(8,128)S(1)}, f32[64,128]{1,0:T(8,128)S(1)}, u32[]{:S(2)}, u32[]{:S(2)}) collective-permute-start(f32[64,128]{1,0:T(8,128)S(1)} %first.1.z_ref.z1_ref), channel_id=1, source_target_pairs={{8,16},{16,8},{9,17},{17,9},{10,18},{18,10},{11,19},{19,11},{12,20... | collective-permute-start | bytes 98312 | tf_op jit(solution)/shard_map/ppermute | solution.py:319
  36.0 0.9 collective-permute-start
  36.9 0.7 collective-permute-start.3
  37.6 0.0 collective-permute-done.2.refs_2_
  37.6 1.6 %collective-permute-done.1.refs_1_ = f32[64,128]{1,0:T(8,128)S(1)} collective-permute-done((f32[64,128]{1,0:T(8,128)S(1)}, f32[64,128]{1,0:T(8,128)S(1)}, u32[]{:S(2)}, u32[]{:S(2)}) %collective-permute-start.1) | collective-permute-done | bytes 32800 | tf_op jit(solution)/shard_map/ppermute | solution.py:319
  39.1 0.0 collective-permute-done.refs_0_
  39.1 0.0 copy-done
  39.2 1.0 %own.2.own_ref = f32[64,128]{1,0:T(8,128)S(1)} custom-call(f32[64,128]{1,0:T(8,128)S(1)} %first.1.z_ref.z1_ref, bf16[64,64,128]{2,1,0:T(8,128)(2,1)S(1)} %copy-done.1, f32[64,128]{1,0:T(8,128)S(1)} %copy-done.2, f32[1,128]{1,0:T(1,128)S(1)} %bitcast.20, s32[4,128]{1,0:T(4,128)S(1)} %copy-done.3, f32[64,128]{1,0:T(8,128)S(1)} %collective-permute-done.refs_0_, ...), custom_call_target="tpu_custom_call" | custom-call | tf_op jit(solution)/shard_map/own/pallas_call | solution.py:322
  40.2 0.0 collective-permute-done.3.refs_0_
  40.2 0.7 image.1
  40.9 22.4 %all_to_all.34 = f32[256,1,128]{2,1,0:T(1,128)S(1)} all-to-all(f32[256,1,128]{2,1,0:T(1,128)S(1)} %bitcast.19), channel_id=1, replica_groups=mesh['gx'=32,'gy'=8] {'gx','gy'}, dimensions={0} | all-to-all | bytes 262144 | tf_op jit(solution)/shard_map/all_to_all | solution.py:294
  63.4 1.2 %second.1 = (f32[64,128]{1,0:T(8,128)S(1)}, f32[64,128]{1,0:T(8,128)S(1)}, f32[8,128]{1,0:T(8,128)S(1)}) custom-call(f32[64,128]{1,0:T(8,128)S(1)} %get-tuple-element.16.refs_2_.b_ref, f32[64,128]{1,0:T(8,128)S(1)} %get-tuple-element.22.w_ref, f32[8,128]{1,0:T(8,128)S(1)} %get-tuple-element.17.mask_ref, f32[64,128]{1,0:T(8,128)S(1)} %first.1.z_ref.z1_ref, ...), custom_call_target="tpu_custom_call" | custom-call | tf_op jit(solution)/shard_map/second/pallas_call | solution.py:332
  64.6 0.7 collective-permute-start.6
  65.3 2.1 %collective-permute-start.5 = (f32[64,128]{1,0:T(8,128)S(1)}, f32[64,128]{1,0:T(8,128)S(1)}, u32[]{:S(2)}, u32[]{:S(2)}) collective-permute-start(f32[64,128]{1,0:T(8,128)S(1)} %get-tuple-element.26.z_ref.z2_ref), channel_id=1, source_target_pairs={{8,16},{16,8},{9,17},{17,9},{10,18},{18,10},{11,19},{19,11},{12,20... | collective-permute-start | bytes 98312 | tf_op jit(solution)/shard_map/ppermute | solution.py:319
  67.4 0.9 collective-permute-start.4
  68.3 0.7 collective-permute-start.7
  68.9 0.0 collective-permute-done.6.refs_2_
  69.0 1.6 %collective-permute-done.5.refs_1_ = f32[64,128]{1,0:T(8,128)S(1)} collective-permute-done((f32[64,128]{1,0:T(8,128)S(1)}, f32[64,128]{1,0:T(8,128)S(1)}, u32[]{:S(2)}, u32[]{:S(2)}) %collective-permute-start.5) | collective-permute-done | bytes 32800 | tf_op jit(solution)/shard_map/ppermute | solution.py:319
  70.5 0.0 collective-permute-done.4.refs_0_
  70.5 1.0 %own.3.own_ref = f32[64,128]{1,0:T(8,128)S(1)} custom-call(f32[64,128]{1,0:T(8,128)S(1)} %get-tuple-element.26.z_ref.z2_ref, bf16[64,64,128]{2,1,0:T(8,128)(2,1)S(1)} %copy-done.1, f32[64,128]{1,0:T(8,128)S(1)} %copy-done.2, f32[1,128]{1,0:T(1,128)S(1)} %bitcast.21, s32[4,128]{1,0:T(4,128)S(1)} %copy-done.3, f32[64,128]{1,0:T(8,128)S(1)} %collective-permute-done.4.refs_0_, ...), custom_call_target="tpu_custom_call" | custom-call | tf_op jit(solution)/shard_map/own/pallas_call | solution.py:322
  71.5 0.0 collective-permute-done.7.refs_0_
  71.5 0.4 last_image.1
  72.0 22.5 %all_to_all.35 = f32[256,1,128]{2,1,0:T(1,128)S(1)} all-to-all(f32[256,1,128]{2,1,0:T(1,128)S(1)} %bitcast.15), channel_id=1, replica_groups=mesh['gx'=32,'gy'=8] {'gx','gy'}, dimensions={0} | all-to-all | bytes 262144 | tf_op jit(solution)/shard_map/all_to_all | solution.py:294
  94.5 0.8 final.1
  (5 shorter events, 0.0 us)
Async XLA Ops:
  1.3 37.9 %copy-start = (bf16[4,64,64,128]{3,2,1,0:T(8,128)(2,1)S(1)}, bf16[4,64,64,128]{3,2,1,0:T(8,128)(2,1)}, u32[]{:S(2)}) copy-start(bf16[4,64,64,128]{3,2,1,0:T(8,128)(2,1)} %refs_1_.3) | copy-start | bytes 12582916
  3.7 35.4 %copy-start.1 = (bf16[64,64,128]{2,1,0:T(8,128)(2,1)S(1)}, bf16[64,64,128]{2,1,0:T(8,128)(2,1)}, u32[]{:S(2)}) copy-start(bf16[64,64,128]{2,1,0:T(8,128)(2,1)} %blocks_ref.3) | copy-start | bytes 3145732
  3.8 35.4 %copy-start.2 = (f32[64,128]{1,0:T(8,128)S(1)}, f32[64,128]{1,0:T(8,128)}, u32[]{:S(2)}) copy-start(f32[64,128]{1,0:T(8,128)} %pressure_ref.3) | copy-start | bytes 98308
  3.8 35.4 %copy-start.3 = (s32[4,128]{1,0:T(4,128)S(1)}, s32[4,128]{1,0:T(4,128)}, u32[]{:S(2)}) copy-start(s32[4,128]{1,0:T(4,128)} %partners_ref.7) | copy-start | bytes 6148
  3.8 35.4 %copy-start.4 = (f32[128]{0:T(128)S(1)}, f32[128]{0:T(128)}, u32[]{:S(2)}) copy-start(f32[128]{0:T(128)} %param.12) | copy-start | bytes 1540
  33.2 4.3 %collective-permute-start.2 = (f32[64,128]{1,0:T(8,128)S(1)}, f32[64,128]{1,0:T(8,128)S(1)}, u32[]{:S(2)}, u32[]{:S(2)}) collective-permute-start(f32[64,128]{1,0:T(8,128)S(1)} %first.1.z_ref.z1_ref), channel_id=1, source_target_pairs={{0,8},{8,0},{1,9},{9,1},{2,10},{10,2},{3,11},{11,3},{4,12},{12,4},... | collective-permute-start | bytes 98312 | tf_op jit(solution)/shard_map/ppermute | solution.py:319
  33.9 5.2 %collective-permute-start.1 = (f32[64,128]{1,0:T(8,128)S(1)}, f32[64,128]{1,0:T(8,128)S(1)}, u32[]{:S(2)}, u32[]{:S(2)}) collective-permute-start(f32[64,128]{1,0:T(8,128)S(1)} %first.1.z_ref.z1_ref), channel_id=1, source_target_pairs={{8,16},{16,8},{9,17},{17,9},{10,18},{18,10},{11,19},{19,11},{12,20... | collective-permute-start | bytes 98312 | tf_op jit(solution)/shard_map/ppermute | solution.py:319
  36.0 3.2 %collective-permute-start = (f32[64,128]{1,0:T(8,128)S(1)}, f32[64,128]{1,0:T(8,128)S(1)}, u32[]{:S(2)}, u32[]{:S(2)}) collective-permute-start(f32[64,128]{1,0:T(8,128)S(1)} %first.1.z_ref.z1_ref), channel_id=1, source_target_pairs={{0,1},{1,0},{2,3},{3,2},{4,5},{5,4},{6,7},{7,6},{8,9},{9,8},{10,11... | collective-permute-start | bytes 98312 | tf_op jit(solution)/shard_map/ppermute | solution.py:319
  36.9 3.3 %collective-permute-start.3 = (f32[64,128]{1,0:T(8,128)S(1)}, f32[64,128]{1,0:T(8,128)S(1)}, u32[]{:S(2)}, u32[]{:S(2)}) collective-permute-start(f32[64,128]{1,0:T(8,128)S(1)} %first.1.z_ref.z1_ref), channel_id=1, source_target_pairs={{1,2},{2,1},{3,4},{4,3},{5,6},{6,5},{9,10},{10,9},{11,12},{12,11},... | collective-permute-start | bytes 98312 | tf_op jit(solution)/shard_map/ppermute | solution.py:319
  64.6 4.3 %collective-permute-start.6 = (f32[64,128]{1,0:T(8,128)S(1)}, f32[64,128]{1,0:T(8,128)S(1)}, u32[]{:S(2)}, u32[]{:S(2)}) collective-permute-start(f32[64,128]{1,0:T(8,128)S(1)} %get-tuple-element.26.z_ref.z2_ref), channel_id=1, source_target_pairs={{0,8},{8,0},{1,9},{9,1},{2,10},{10,2},{3,11},{11,3},{4,12},{12,4},... | collective-permute-start | bytes 98312 | tf_op jit(solution)/shard_map/ppermute | solution.py:319
  65.3 5.2 %collective-permute-start.5 = (f32[64,128]{1,0:T(8,128)S(1)}, f32[64,128]{1,0:T(8,128)S(1)}, u32[]{:S(2)}, u32[]{:S(2)}) collective-permute-start(f32[64,128]{1,0:T(8,128)S(1)} %get-tuple-element.26.z_ref.z2_ref), channel_id=1, source_target_pairs={{8,16},{16,8},{9,17},{17,9},{10,18},{18,10},{11,19},{19,11},{12,20... | collective-permute-start | bytes 98312 | tf_op jit(solution)/shard_map/ppermute | solution.py:319
  67.4 3.2 %collective-permute-start.4 = (f32[64,128]{1,0:T(8,128)S(1)}, f32[64,128]{1,0:T(8,128)S(1)}, u32[]{:S(2)}, u32[]{:S(2)}) collective-permute-start(f32[64,128]{1,0:T(8,128)S(1)} %get-tuple-element.26.z_ref.z2_ref), channel_id=1, source_target_pairs={{0,1},{1,0},{2,3},{3,2},{4,5},{5,4},{6,7},{7,6},{8,9},{9,8},{10,11... | collective-permute-start | bytes 98312 | tf_op jit(solution)/shard_map/ppermute | solution.py:319
  68.3 3.2 %collective-permute-start.7 = (f32[64,128]{1,0:T(8,128)S(1)}, f32[64,128]{1,0:T(8,128)S(1)}, u32[]{:S(2)}, u32[]{:S(2)}) collective-permute-start(f32[64,128]{1,0:T(8,128)S(1)} %get-tuple-element.26.z_ref.z2_ref), channel_id=1, source_target_pairs={{1,2},{2,1},{3,4},{4,3},{5,6},{6,5},{9,10},{10,9},{11,12},{12,11},... | collective-permute-start | bytes 98312 | tf_op jit(solution)/shard_map/ppermute | solution.py:319
